TPU v7x, 32 devices: a whole 2x2x4 slice. The times are simulated.
32 devices in a mesh: dp: 16 (over z, y, core), mp: 2 (over x).
Axes of the slice: x: 2, y: 2, z: 4, core: 2. Of those that a mesh axis runs over, the one named last changes fastest.
Arguments:
- tokens: bfloat16 [1024, 5120], P('dp', 'mp'), may hold values from -6 to 6, as said below
- gate_first: bfloat16 [13824, 5120], P('dp', 'mp'), may hold values from -6 to 6
- up_first: bfloat16 [13824, 5120], P('dp', 'mp'), may hold values from -6 to 6
- down_first: bfloat16 [13824, 5120], P('dp', 'mp'), may hold values from -6 to 6
- gate_second: bfloat16 [13824, 5120], P('dp', 'mp'), may hold values from -6 to 6
- up_second: bfloat16 [13824, 5120], P('dp', 'mp'), may hold values from -6 to 6
- down_second: bfloat16 [13824, 5120], P('dp', 'mp'), may hold values from -6 to 6
- matching: int32 [13824], replicated, may hold values from 0 to 13823, as said below
Outputs:
- merged_gate: bfloat16 [13824, 5120], P('dp', 'mp')
- merged_up: bfloat16 [13824, 5120], P('dp', 'mp')
- merged_down: bfloat16 [13824, 5120], P('dp', 'mp')
- correlation: float32 [3456, 13824], P('mp', 'dp')
Inputs may be any that keep to these rules, and one draw needn't show every extreme that they name: matching is a permutation; for any aligned block of 864 positions and any aligned block of 864 values, at most 54 of the block's entries lie in that block of values, and in every draw some pair of blocks holds exactly 54. `tokens`: each token's 5120 features have a mean square within a few hundredths of 1.
All inputs are finite; a program needn't handle non-finite values.
Results may differ from a plain program's by a relative error of at most 0.028.
Values may be sent and summed in bfloat16 or wider, within the bound.
A program may use at most 128 MiB of HBM per device.

v0:
```python
import math

import jax
import jax.numpy as jnp
from jax import lax
from jax.sharding import PartitionSpec as P

D = 5120
CROWS = 216


def local(tokens, gate_first, up_first, down_first, gate_second, up_second, down_second, matching):
    data_size = lax.axis_size("dp")
    model_size = lax.axis_size("mp")
    position = lax.axis_index("dp")
    unit_count = gate_first.shape[0]
    feature_cols = gate_first.shape[1]
    capacity = -(-unit_count // data_size)
    everyone = lax.all_gather(tokens, "dp", axis=0, tiled=True)
    token_count = everyone.shape[0]
    row_count = token_count // model_size
    stacked = jnp.concatenate([gate_first, up_first, gate_second, up_second], axis=0)
    factor = 1.0 / math.sqrt(D)
    block = everyone
    preact = lax.psum_scatter(
        (
            lax.dot_general(
                block, stacked, (((1,), (1,)), ((), ())), preferred_element_type=jnp.float32
            )
            * factor
        ).astype(jnp.bfloat16),
        "mp",
        scatter_dimension=0,
        tiled=True,
    ).astype(jnp.float32)
    gate_one = preact[:, :unit_count]
    up_one = preact[:, unit_count : 2 * unit_count]
    gate_two = preact[:, 2 * unit_count : 3 * unit_count]
    up_two = preact[:, 3 * unit_count :]
    hidden_first = (jax.nn.silu(gate_one) * up_one).astype(jnp.bfloat16)
    hidden_second = (jax.nn.silu(gate_two) * up_two).astype(jnp.bfloat16)
    routing = matching.reshape(data_size, unit_count)
    owners = routing // unit_count
    offsets = routing % unit_count
    owned = owners == position
    ranking = jnp.cumsum(owned.astype(jnp.int32), axis=1) - 1
    slot_ids = jnp.arange(capacity, dtype=jnp.int32)
    matches = owned[:, None, :] & (ranking[:, None, :] == slot_ids[None, :, None])
    send_index = jnp.sum(jnp.where(matches, offsets[:, None, :], 0), axis=2).reshape(-1)
    sources = lax.dynamic_slice_in_dim(matching, position * unit_count, unit_count)
    source_block = sources // unit_count
    order_ids = jnp.arange(unit_count, dtype=jnp.int32)
    earlier = (source_block[None, :] == source_block[:, None]) & (
        order_ids[None, :] < order_ids[:, None]
    )
    arrival = jnp.sum(earlier.astype(jnp.int32), axis=1)
    landing = source_block * capacity + arrival
    second_rows = jnp.concatenate([gate_second, up_second, down_second], axis=1)
    outgoing = jnp.take(second_rows, send_index, axis=0).reshape(
        data_size, capacity, 3 * feature_cols
    )
    incoming = lax.all_to_all(outgoing, "dp", split_axis=0, concat_axis=0, tiled=True)
    moved = jnp.take(incoming.reshape(data_size * capacity, 3 * feature_cols), landing, axis=0)

    def averaged(first, second):
        return ((first.astype(jnp.float32) + second.astype(jnp.float32)) * 0.5).astype(jnp.bfloat16)

    merged_gate = averaged(gate_first, moved[:, :feature_cols])
    merged_up = averaged(up_first, moved[:, feature_cols : 2 * feature_cols])
    merged_down = averaged(down_first, moved[:, 2 * feature_cols :])
    window_all = lax.all_gather(hidden_first[:, :CROWS], "dp", axis=1, tiled=True)
    flipped = hidden_second.T
    outgoing_second = jnp.take(flipped, send_index, axis=0).reshape(data_size, capacity, row_count)
    incoming_second = lax.all_to_all(outgoing_second, "dp", split_axis=0, concat_axis=0, tiled=True)
    chosen = jnp.take(incoming_second.reshape(data_size * capacity, row_count), landing, axis=0).T
    block = window_all
    summed = lax.psum_scatter(
        lax.dot_general(
            block, chosen, (((0,), (0,)), ((), ())), preferred_element_type=jnp.float32
        ).astype(jnp.bfloat16),
        "mp",
        scatter_dimension=0,
        tiled=True,
    ).astype(jnp.float32)
    correlation = summed / math.sqrt(token_count)
    return (merged_gate, merged_up, merged_down, correlation)


def solution(mesh):
    in_specs = (
        P("dp", "mp"),
        P("dp", "mp"),
        P("dp", "mp"),
        P("dp", "mp"),
        P("dp", "mp"),
        P("dp", "mp"),
        P("dp", "mp"),
        P(),
    )
    out_specs = (P("dp", "mp"), P("dp", "mp"), P("dp", "mp"), P("mp", "dp"))
    return jax.shard_map(local, mesh=mesh, in_specs=in_specs, out_specs=out_specs, check_vma=False)
```

profile of v0, /device:TPU:13, one launch (start us, length us, event | category | flops | bytes accessed | tf_op | source)
XLA Modules:
  0.0 622.0 jit_solution(2835680632450477860)
XLA Ops:
  7.2 0.0 all-gather.3.cloned.1.call-start
  7.2 0.7 all-gather.3.cloned.1.call-update
  7.9 0.0 reduce-scatter.3.cloned.1.call-start
  7.9 58.7 %all-gather.3.cloned.1.call-done = bf16[1024,2560]{1,0:T(8,128)(2,1)} async-done(((bf16[64,2560]{1,0:T(8,128)(2,1)}), bf16[1024,2560]{1,0:T(8,128)(2,1)}) %all-gather.3.cloned.1.call-update) | async-done | bytes 5242896 | tf_op jit(solution)/shard_map/all_gather | solution.py:19
  66.7 31.9 %fusion.10 = bf16[1024,3456]{0,1:T(8,128)(2,1)} fusion(bf16[1024,2560]{1,0:T(8,128)(2,1)} %all-gather.3.cloned.1.call-done, bf16[864,2560]{1,0:T(8,128)(2,1)} %param.17, bf16[864,2560]{1,0:T(8,128)(2,1)} %param.16, bf16[864,2560]{1,0:T(8,128)(2,1)} %param.14, bf16[864,2560]{1,0:T(8,128)(2,1)} %param.13), kind=kOutput, calls=%fused_computation.20 | convolution fusion | flops 18197250048 | bytes 30015488 | tf_op jit(solution)/shard_map/dot_general | solution.py:27
  98.5 0.0 reduce-scatter.3.cloned.1.call-update
  98.6 0.8 copy-done.1
  99.4 0.1 rem.34
  99.5 0.1 div.33
  99.6 0.1 ne.58
  99.8 2.0 reduce-window.6
  101.8 0.3 slice_reduce_fusion
  102.1 0.1 copy_bitcast_fusion
  102.2 1.0 select_reduce_fusion
  103.2 0.1 copy.18
  103.3 0.1 reshape.83
  103.4 11.2 %pad_maximum_fusion = bf16[864,7680]{1,0:T(8,128)(2,1)} fusion(bf16[864,2560]{1,0:T(8,128)(2,1)} %param.18, bf16[864,2560]{1,0:T(8,128)(2,1)} %param.17, bf16[864,2560]{1,0:T(8,128)(2,1)} %param.16), kind=kLoop, calls=%fused_computation.13 | loop fusion | flops 39813120 | bytes 26542080 | tf_op jit(solution)/shard_map/concatenate | solution.py:58
  114.6 33.7 %gather_fusion = bf16[864,7680]{1,0:T(8,128)(2,1)} fusion(bf16[864,7680]{1,0:T(8,128)(2,1)} %pad_maximum_fusion, s32[1024]{0:T(1024)S(1)} %pad_clamp_fusion.1), kind=kCustom, calls=%fused_computation.clone | custom fusion | bytes 26545536 | tf_op jit(solution)/shard_map/jit(_take)/gather | solution.py:59
  148.3 35.1 %reduce-scatter.3.cloned.1.call-done = bf16[512,3456]{0,1:T(8,128)(2,1)} async-done(((bf16[1024,3456]{0,1:T(8,128)(2,1)}), bf16[512,3456]{0,1:T(8,128)(2,1)}) %reduce-scatter.3.cloned.1.call-update) | async-done | bytes 3538960 | tf_op jit(solution)/shard_map/reduce_scatter | solution.py:25
  183.4 3.1 convert_element_type.64
  186.5 0.0 copy-done
  186.5 2.8 fusion.18
  189.3 3.5 gather_fusion.2
  192.8 0.2 broadcast_select_fusion.2
  193.0 1.2 reshape.86
  194.2 6.5 %all-to-all-start.1 = ((bf16[16,54,512]{2,1,0:T(8,128)(2,1)}), bf16[16,54,512]{2,1,0:T(8,128)(2,1)S(1)}, u32[]{:S(2)}, u32[]{:S(2)}) async-start(bf16[16,54,512]{2,1,0:T(8,128)(2,1)} %reshape.86), calls=%async_computation.2 | async-start | bytes 1835008 | tf_op jit(solution)/shard_map/all_to_all | solution.py:74
  200.6 11.2 %broadcast_select_fusion.1 = bf16[864,7680]{1,0:T(8,128)(2,1)} fusion(bf16[864,7680]{1,0:T(8,128)(2,1)} %gather_fusion, pred[864]{0:T(1024)(128)(4,1)S(1)} %compare_and_fusion.1), kind=kLoop, calls=%fused_computation.15 | loop fusion | flops 6635520 | bytes 26542944 | tf_op jit(solution)/shard_map/jit(_take)/select_n | solution.py:59
  211.8 11.3 %reshape.84 = bf16[16,54,7680]{2,1,0:T(8,128)(2,1)} reshape(bf16[864,7680]{1,0:T(8,128)(2,1)} %broadcast_select_fusion.1) | data formatting | bytes 26542080 | tf_op jit(solution)/shard_map/reshape | solution.py:59
  223.1 0.0 all-to-all-done.1
  223.1 6.0 all-to-all-start
  229.1 0.0 all-gather.5.cloned.1.call-start
  229.2 2.1 fusion.19
  231.3 0.0 all-gather.5.cloned.1.call-update
  231.3 0.0 reduce-scatter.5.cloned.1.call-start
  231.3 0.1 add_select_fusion.2
  231.4 0.4 convert_reduce_fusion
  231.9 0.1 compare_and_fusion
  232.0 0.2 reshape.87
  232.2 3.7 gather_fusion.3
  235.9 194.4 %all-gather.5.cloned.1.call-done = bf16[512,3456]{0,1:T(8,128)(2,1)} async-done(((bf16[512,216]{0,1:T(8,128)(2,1)}), bf16[512,3456]{0,1:T(8,128)(2,1)}) %all-gather.5.cloned.1.call-update) | async-done | bytes 3538960 | tf_op jit(solution)/shard_map/all_gather | solution.py:71
  430.2 8.6 %convolution_convert_fusion = bf16[3456,864]{1,0:T(8,128)(2,1)} fusion(bf16[512,3456]{0,1:T(8,128)(2,1)} %all-gather.5.cloned.1.call-done, bf16[864,512]{1,0:T(8,128)(2,1)S(1)} %gather_fusion.3, pred[864]{0:T(1024)(128)(4,1)S(1)} %get-tuple-element.6), kind=kOutput, calls=%fused_computation.19 | convolution fusion | flops 3061075968 | bytes 10396512 | tf_op jit(solution)/shard_map/dot_general | solution.py:78
  438.9 0.0 reduce-scatter.5.cloned.1.call-update
  438.9 109.1 %all-to-all-done = bf16[16,54,7680]{2,1,0:T(8,128)(2,1)} async-done(((bf16[16,54,7680]{2,1,0:T(8,128)(2,1)}), bf16[16,54,7680]{2,1,0:T(8,128)(2,1)}, u32[]{:S(2)}, u32[]{:S(2)}) %all-to-all-start) | async-done | bytes 13271072 | tf_op jit(solution)/shard_map/all_to_all | solution.py:62
  548.0 11.2 %reshape.85 = bf16[864,7680]{1,0:T(8,128)(2,1)} reshape(bf16[16,54,7680]{2,1,0:T(8,128)(2,1)} %all-to-all-done) | data formatting | bytes 26542080 | tf_op jit(solution)/shard_map/reshape | solution.py:63
  559.2 33.0 %gather_fusion.1 = bf16[864,7680]{1,0:T(8,128)(2,1)} fusion(bf16[864,7680]{1,0:T(8,128)(2,1)} %reshape.85, s32[1024]{0:T(1024)S(1)} %pad_clamp_fusion), kind=kCustom, calls=%fused_computation.2.clone | custom fusion | bytes 26545536 | tf_op jit(solution)/shard_map/jit(_take)/gather | solution.py:63
  592.2 6.7 %broadcast_select_fusion = bf16[864,7680]{1,0:T(8,128)(2,1)S(1)} fusion(bf16[864,7680]{1,0:T(8,128)(2,1)} %gather_fusion.1, pred[864]{0:T(1024)(128)(4,1)S(1)} %get-tuple-element.6), kind=kLoop, calls=%fused_computation.14 | loop fusion | flops 6635520 | bytes 26542944 | tf_op jit(solution)/shard_map/jit(_take)/select_n | solution.py:63
  598.9 11.4 %multiply_convert_fusion.1 = (bf16[864,2560]{1,0:T(8,128)(2,1)}, bf16[864,2560]{1,0:T(8,128)(2,1)}, bf16[864,2560]{1,0:T(8,128)(2,1)}) fusion(bf16[864,2560]{1,0:T(8,128)(2,1)} %param.15, bf16[864,7680]{1,0:T(8,128)(2,1)S(1)} %broadcast_select_fusion, bf16[864,2560]{1,0:T(8,128)(2,1)} %param.14, bf16[864,2560]{1,0:T(8,128)(2,1)} %param.13), kind=kLoop, calls=%fused_computation.16 | loop fusion | flops 33177600 | bytes 39813120 | tf_op jit(solution)/shard_map/convert_element_type | solution.py:66
  610.3 4.9 convert_multiply_fusion
  (13 shorter events, 0.2 us)
Async XLA Ops:
  7.2 59.5 %all-gather.3.cloned.1.call-start = ((), (), s32[]{:S(2)}) async-start(), calls=%async_computation.4 | async-start | bytes 5570560 | tf_op jit(solution)/shard_map/all_gather | solution.py:19
  7.9 175.5 %reduce-scatter.3.cloned.1.call-start = ((), (), s32[]{:S(2)}) async-start(), calls=%async_computation.5 | async-start | bytes 10616832 | tf_op jit(solution)/shard_map/reduce_scatter | solution.py:25
  98.5 0.8 copy-start.1
  183.4 3.2 copy-start
  194.2 28.9 %all-to-all-start.1 = ((bf16[16,54,512]{2,1,0:T(8,128)(2,1)}), bf16[16,54,512]{2,1,0:T(8,128)(2,1)S(1)}, u32[]{:S(2)}, u32[]{:S(2)}) async-start(bf16[16,54,512]{2,1,0:T(8,128)(2,1)} %reshape.86), calls=%async_computation.2 | async-start | bytes 1835008 | tf_op jit(solution)/shard_map/all_to_all | solution.py:74
  223.1 324.9 %all-to-all-start = ((bf16[16,54,7680]{2,1,0:T(8,128)(2,1)}), bf16[16,54,7680]{2,1,0:T(8,128)(2,1)}, u32[]{:S(2)}, u32[]{:S(2)}) async-start(bf16[16,54,7680]{2,1,0:T(8,128)(2,1)} %reshape.84), calls=%async_computation | async-start | bytes 27525120 | tf_op jit(solution)/shard_map/all_to_all | solution.py:62
  229.1 201.1 %all-gather.5.cloned.1.call-start = ((), (), s32[]{:S(2)}) async-start(), calls=%async_computation.6 | async-start | bytes 3760128 | tf_op jit(solution)/shard_map/all_gather | solution.py:71
  231.3 379.0 %reduce-scatter.5.cloned.1.call-start = ((), (), s32[]{:S(2)}) async-start(), calls=%async_computation.7 | async-start | bytes 9289728 | tf_op jit(solution)/shard_map/reduce_scatter | solution.py:77
Sparse Core Ops, SparseCore 0:
  10.3 56.3 all-gather.2
  98.7 84.6 reduce-scatter.2
  232.8 197.4 all-gather.4
  439.0 73.6 reduce-scatter.4
where the time goes:
time: 630 us; the launch traced here: 622 us
  waiting for transfers between devices  398 us (63%)
  local copies, waits for them, and re-layouts  99.3 us (16%)
  other arithmetic  57.5 us (9%)
  matrix products  40.5 us (6%)
  between operations  14.1 us (2%)
  starting transfers between devices  12.6 us (2%)
    all_gather x1, waiting for transfers between devices, local(): lax.all_gather(hidden_first[:, :CROWS], 'dp', axis=1, tiled=True)  194 us
    all_to_all x1, waiting for transfers between devices, local(): lax.all_to_all(outgoing, 'dp', split_axis=0, concat_axis=0, tiled=True)  109 us
    all_gather x1, waiting for transfers between devices, local(): everyone = lax.all_gather(tokens, 'dp', axis=0, tiled=True)  58.7 us
    reduce_scatter x1, waiting for transfers between devices, local(): lax.psum_scatter((lax.dot_general(block, stacked, (((1,), (1,)), ((), ())...  35.1 us
    gather x1, local copies, waits for them, and re-layouts, local(): jnp.take(second_rows, send_index, axis=0)  33.7 us
    gather x1, local copies, waits for them, and re-layouts, local(): jnp.take(incoming.reshape(data_size * capacity, 3 * feature_cols), landin...  33 us
    dot_general x1, matrix products, local(): lax.dot_general(block, stacked, (((1,), (1,)), ((), ())), preferred_eleme...  31.9 us
  transfers between devices with their start and end apart: 6, of which 4 were waited for; matrix products, arithmetic and copies ran while one was open for 24% of the time, Pallas kernels for 0%

commit v1 on v0

v1 whole, which is shorter than its diff:
```python
import math

import jax
import jax.numpy as jnp
from jax import lax
from jax.sharding import PartitionSpec as P

D = 5120
CROWS = 216


def matmul_t(a, b):
    return lax.dot_general(a, b, (((1,), (1,)), ((), ())), preferred_element_type=jnp.float32)


def pick(onehot, rows):
    return jnp.dot(onehot, rows, preferred_element_type=jnp.float32).astype(jnp.bfloat16)


def local(tokens, gate_first, up_first, down_first, gate_second, up_second, down_second, matching):
    data_size = lax.axis_size("dp")
    model_size = lax.axis_size("mp")
    position = lax.axis_index("dp")
    unit_count = gate_first.shape[0]
    feature_cols = gate_first.shape[1]
    capacity = -(-unit_count // data_size)
    slots = data_size * capacity
    factor = 1.0 / math.sqrt(D)

    everyone = lax.all_gather(tokens, "dp", axis=0, tiled=True)
    token_count = everyone.shape[0]

    routing = matching.reshape(data_size, unit_count)
    owners = lax.div(routing, unit_count)
    offsets = routing - owners * unit_count
    owned = owners == position
    unit_ids = jnp.arange(unit_count, dtype=jnp.int32)
    before = (unit_ids[:, None] < unit_ids[None, :]).astype(jnp.bfloat16)
    ranking = jnp.dot(owned.astype(jnp.bfloat16), before, preferred_element_type=jnp.float32)
    ranking = ranking.astype(jnp.int32)
    slot_ids = jnp.arange(capacity, dtype=jnp.int32)
    matches = owned[:, None, :] & (ranking[:, None, :] == slot_ids[None, :, None])
    send_index = jnp.sum(jnp.where(matches, offsets[:, None, :], 0), axis=2).reshape(-1)
    chooser = (send_index[:, None] == unit_ids[None, :]).astype(jnp.bfloat16)

    sources = lax.dynamic_slice_in_dim(matching, position * unit_count, unit_count)
    source_block = lax.div(sources, unit_count)
    earlier = (source_block[None, :] == source_block[:, None]) & (
        unit_ids[None, :] < unit_ids[:, None]
    )
    landing = source_block * capacity + jnp.sum(earlier.astype(jnp.int32), axis=1)
    placer = (landing[:, None] == jnp.arange(slots, dtype=jnp.int32)[None, :]).astype(jnp.bfloat16)

    def exchange(rows):
        return lax.all_to_all(
            rows.reshape(data_size, capacity, -1), "dp", split_axis=0, concat_axis=0, tiled=True
        ).reshape(slots, -1)

    def averaged(first, moved):
        return ((first.astype(jnp.float32) + moved.astype(jnp.float32)) * 0.5).astype(jnp.bfloat16)

    def hidden(rows):
        count = rows.shape[0] // 2
        term = (matmul_t(everyone, rows) * factor).astype(jnp.bfloat16)
        parts = lax.all_to_all(
            term.reshape(model_size, -1, 2 * count), "mp", split_axis=0, concat_axis=0, tiled=True
        )
        pre = jnp.sum(parts.astype(jnp.float32), axis=0)
        return (jax.nn.silu(pre[:, :count]) * pre[:, count:]).astype(jnp.bfloat16)

    gate_out = pick(chooser, gate_second)
    up_out = pick(chooser, up_second)
    gate_in = exchange(gate_out)
    up_in = exchange(up_out)
    down_out = pick(chooser, down_second)

    window = hidden(jnp.concatenate([gate_first[:CROWS], up_first[:CROWS]], axis=0))
    window = lax.all_gather(window, "dp", axis=1, tiled=True)
    window = lax.all_to_all(window, "mp", split_axis=1, concat_axis=0, tiled=True)

    down_out, up_in, gate_in = lax.optimization_barrier((down_out, up_in, gate_in))
    down_in = exchange(down_out)
    gate_moved = pick(placer, gate_in)
    up_moved = pick(placer, up_in)
    chosen = hidden(jnp.concatenate([gate_moved, up_moved], axis=0))
    chosen = lax.all_gather(chosen, "mp", axis=0, tiled=True)
    merged_gate = averaged(gate_first, gate_moved)
    merged_up = averaged(up_first, up_moved)
    merged_down = averaged(down_first, pick(placer, down_in))
    correlation = lax.dot_general(
        window, chosen, (((0,), (0,)), ((), ())), preferred_element_type=jnp.float32
    ) / math.sqrt(token_count)
    return (merged_gate, merged_up, merged_down, correlation)


def solution(mesh):
    in_specs = (P("dp", "mp"),) * 7 + (P(),)
    out_specs = (P("dp", "mp"), P("dp", "mp"), P("dp", "mp"), P("mp", "dp"))
    return jax.shard_map(local, mesh=mesh, in_specs=in_specs, out_specs=out_specs, check_vma=False)
```

time: 630 us -> 575 us (0.913)
  local copies, waits for them, and re-layouts: 99.3 us -> 40.7 us
  other arithmetic: 57.5 us -> 11.3 us
  matrix products: 40.5 us -> 82.2 us
  starting transfers between devices: 12.6 us -> 29.3 us
    all_to_all x2 -> x6, waiting for transfers between devices: 109 us -> 395 us  [the longest x3 320 us: exchange(): lax.all_to_all(rows.reshape(data_size, capacity, -1), 'dp', split_axis=0,...]
    all_gather x1 -> x2, waiting for transfers between devices: 194 us -> 0.01 us  [the longest x1 0.01 us: local(): window = lax.all_gather(window, 'dp', axis=1, tiled=True)]
    gather x4 -> x0, local copies, waits for them, and re-layouts: 73.9 us -> none  [the longest x1 33.7 us: local(): jnp.take(second_rows, send_index, axis=0)]
    all_gather x1, waiting for transfers between devices: 58.7 us -> 0.01 us  [local(): everyone = lax.all_gather(tokens, 'dp', axis=0, tiled=True)]
    dot_general x2 -> x10, matrix products: 40.5 us -> 82.2 us  [the longest x6 53.7 us: pick(): jnp.dot(onehot, rows, preferred_element_type=jnp.float32)]
    reduce_scatter x2 -> x0, waiting for transfers between devices: 35.1 us -> none  [the longest x1 35.1 us: local(): lax.psum_scatter((lax.dot_general(block, stacked, (((1,), (1,)), ((), ())...]
    select_n x6 -> x0, other arithmetic: 18.1 us -> none  [the longest x2 11.2 us: local(): jnp.take(second_rows, send_index, axis=0)]
    all_to_all x2 -> x6, starting transfers between devices: 12.5 us -> 28.7 us  [the longest x3 16.9 us: exchange(): lax.all_to_all(rows.reshape(data_size, capacity, -1), 'dp', split_axis=0,...]
  transfers between devices with their start and end apart: 6 -> 9, of which waited for: 4 -> 5; matrix products, arithmetic and copies ran while one was open for 24% -> 18% of each run, Pallas kernels for 0% -> 0%
where the time goes in v1:
time: 575 us; the launch traced here: 573 us
  waiting for transfers between devices  396 us (69%)
  matrix products  82.2 us (14%)
  local copies, waits for them, and re-layouts  40.7 us (7%)
  starting transfers between devices  29.3 us (5%)
  between operations  13.9 us (2%)
  other arithmetic  11.3 us (2%)
    all_to_all x3, waiting for transfers between devices, exchange(): lax.all_to_all(rows.reshape(data_size, capacity, -1), 'dp', split_axis=0,...  320 us
    dot_general x6, matrix products, pick(): jnp.dot(onehot, rows, preferred_element_type=jnp.float32)  53.7 us
    all_to_all x1, waiting for transfers between devices, local(): lax.all_to_all(window, 'mp', split_axis=1, concat_axis=0, tiled=True)  40.1 us
    all_to_all x2, waiting for transfers between devices, hidden(): lax.all_to_all(term.reshape(model_size, -1, 2 * count), 'mp', split_axis=...  34.9 us
    dot_general x2, matrix products, matmul_t(): lax.dot_general(a, b, (((1,), (1,)), ((), ())), preferred_element_type=jn...  18.9 us
    all_to_all x3, starting transfers between devices, exchange(): lax.all_to_all(rows.reshape(data_size, capacity, -1), 'dp', split_axis=0,...  16.9 us
    reshape x3, local copies, waits for them, and re-layouts, exchange(): return lax.all_to_all(rows.reshape(data_size, capacity, -1), 'dp', split_...  16 us
    reshape x3, local copies, waits for them, and re-layouts, exchange(): rows.reshape(data_size, capacity, -1)  15.9 us
  transfers between devices with their start and end apart: 9, of which 5 were waited for; matrix products, arithmetic and copies ran while one was open for 18% of the time, Pallas kernels for 0%

profile of v1, /device:TPU:13, one launch (start us, length us, event | category | flops | bytes accessed | tf_op | source)
XLA Modules:
  0.0 572.9 jit_solution(245631623053059757)
XLA Ops:
  7.2 0.9 reshape.57
  8.2 0.3 fusion.22
  8.4 1.0 select_reduce_fusion
  9.5 0.1 copy.21
  9.5 0.1 eq.70
  9.6 8.7 %convolution_convert_fusion.4 = bf16[864,2560]{1,0:T(8,128)(2,1)} fusion(bf16[864,2560]{1,0:T(8,128)(2,1)} %param.13, s32[864]{0:T(1024)S(1)} %eq.70), kind=kOutput, calls=%fused_computation.13 | convolution fusion | flops 3825017856 | bytes 8850816 | tf_op jit(solution)/shard_map/dot_general | solution.py:17
  18.4 5.3 reshape.58
  23.7 6.5 %all-to-all-start = ((bf16[16,54,2560]{2,1,0:T(8,128)(2,1)}), bf16[16,54,2560]{2,1,0:T(8,128)(2,1)}, u32[]{:S(2)}, u32[]{:S(2)}) async-start(bf16[16,54,2560]{2,1,0:T(8,128)(2,1)} %reshape.58), calls=%async_computation | async-start | bytes 9175040 | tf_op jit(solution)/shard_map/all_to_all | solution.py:55
  30.2 8.7 %convolution_convert_fusion.3 = bf16[864,2560]{1,0:T(8,128)(2,1)} fusion(bf16[864,2560]{1,0:T(8,128)(2,1)} %param.12, s32[864]{0:T(1024)S(1)} %eq.70), kind=kOutput, calls=%fused_computation.12 | convolution fusion | flops 3825017856 | bytes 8850816 | tf_op jit(solution)/shard_map/dot_general | solution.py:17
  38.9 5.3 reshape.60
  44.2 86.9 %all-to-all-done = bf16[16,54,2560]{2,1,0:T(8,128)(2,1)} async-done(((bf16[16,54,2560]{2,1,0:T(8,128)(2,1)}), bf16[16,54,2560]{2,1,0:T(8,128)(2,1)}, u32[]{:S(2)}, u32[]{:S(2)}) %all-to-all-start) | async-done | bytes 4423712 | tf_op jit(solution)/shard_map/all_to_all | solution.py:55
  131.1 4.8 all-to-all-start.1
  135.9 0.2 all-gather.4.cloned.1.call-start
  136.1 0.5 all-gather.4.cloned.1.call-update
  136.6 0.8 dynamic-slice_divide_fusion
  137.4 0.4 convert_reduce_fusion.1
  137.8 0.8 multiply_add_fusion
  138.6 8.7 %convolution_convert_fusion.5 = bf16[864,2560]{1,0:T(8,128)(2,1)} fusion(bf16[864,2560]{1,0:T(8,128)(2,1)} %param.14, s32[864]{0:T(1024)S(1)} %eq.70), kind=kOutput, calls=%fused_computation.14 | convolution fusion | flops 3825017856 | bytes 8850816 | tf_op jit(solution)/shard_map/dot_general | solution.py:17
  147.4 5.4 reshape.59
  152.7 115.7 %all-to-all-done.1 = bf16[16,54,2560]{2,1,0:T(8,128)(2,1)} async-done(((bf16[16,54,2560]{2,1,0:T(8,128)(2,1)}), bf16[16,54,2560]{2,1,0:T(8,128)(2,1)}, u32[]{:S(2)}, u32[]{:S(2)}) %all-to-all-start.1) | async-done | bytes 4423712 | tf_op jit(solution)/shard_map/all_to_all | solution.py:55
  268.4 5.3 reshape.61
  273.7 10.3 %multiply_convert_fusion.1 = (bf16[864,2560]{1,0:T(8,128)(2,1)}, bf16[864,2560]{1,0:T(8,128)(2,1)}) fusion(bf16[864,2560]{1,0:T(8,128)(2,1)} %param.10, bf16[864,2560]{1,0:T(8,128)(2,1)} %reshape.59, s32[864]{0:T(1024)S(1)} %multiply_add_fusion), kind=kOutput, calls=%fused_computation.5 | convolution fusion | flops 3836077056 | bytes 17698176 | tf_op jit(solution)/shard_map/dot_general | solution.py:17
  284.1 7.2 %multiply_convert_fusion.2 = (bf16[864,2560]{1,0:T(8,128)(2,1)}, bf16[864,2560]{1,0:T(8,128)(2,1)}) fusion(bf16[864,2560]{1,0:T(8,128)(2,1)S(1)} %bitcast.30, bf16[864,2560]{1,0:T(8,128)(2,1)S(1)} %copy-done, s32[864]{0:T(1024)S(1)} %multiply_add_fusion), kind=kOutput, calls=%fused_computation.6 | convolution fusion | flops 3836077056 | bytes 17698176 | tf_op jit(solution)/shard_map/dot_general | solution.py:17
  291.3 5.0 multiply_convert_fusion.4
  296.3 1.0 copy.34
  297.2 3.8 all-to-all-start.3
  301.0 14.0 %multiply_convert_fusion.3 = bf16[1728,1024]{1,0:T(8,128)(2,1)S(1)} fusion(bf16[1024,2560]{1,0:T(8,128)(2,1)} %all-gather.4.cloned.1.call-done, bf16[864,2560]{1,0:T(8,128)(2,1)} %get-tuple-element.13, bf16[864,2560]{1,0:T(8,128)(2,1)} %get-tuple-element.11), kind=kOutput, calls=%fused_computation.8 | convolution fusion | flops 9080930304 | bytes 17629184 | tf_op jit(solution)/shard_map/dot_general | solution.py:13
  315.0 2.0 copy.33
  317.0 1.0 copy-done.1
  318.0 4.0 all-to-all-start.5
  322.0 5.3 reshape.62
  327.3 34.9 %all-to-all-done.5 = bf16[2,512,1728]{1,2,0:T(8,128)(2,1)S(1)} async-done(((bf16[2,512,1728]{1,2,0:T(8,128)(2,1)}), bf16[2,512,1728]{1,2,0:T(8,128)(2,1)S(1)}, u32[]{:S(2)}, u32[]{:S(2)}) %all-to-all-start.5) | async-done | bytes 3538976 | tf_op jit(solution)/shard_map/all_to_all | solution.py:65
  362.2 5.6 all-to-all-start.2
  367.9 0.0 all-gather.6.cloned.1.call-start
  367.9 1.4 convert_reduce_fusion.2
  369.3 0.8 fusion.23
  370.2 0.0 all-gather.6.cloned.1.call-update
  370.2 2.5 convert_reduce_fusion
  372.7 117.5 %all-to-all-done.2 = bf16[16,54,2560]{2,1,0:T(8,128)(2,1)} async-done(((bf16[16,54,2560]{2,1,0:T(8,128)(2,1)}), bf16[16,54,2560]{2,1,0:T(8,128)(2,1)}, u32[]{:S(2)}, u32[]{:S(2)}) %all-to-all-start.2) | async-done | bytes 4423712 | tf_op jit(solution)/shard_map/all_to_all | solution.py:55
  490.1 4.0 all-to-all-start.4
  494.1 0.3 all-gather.8.cloned.1.call-start
  494.4 3.5 fusion.13
  498.0 0.0 all-gather.8.cloned.1.call-update
  498.0 5.3 reshape.63
  503.3 10.0 %multiply_convert_fusion = bf16[864,2560]{1,0:T(8,128)(2,1)} fusion(bf16[864,2560]{1,0:T(8,128)(2,1)} %param.11, bf16[864,2560]{1,0:T(8,128)(2,1)} %reshape.63, s32[864]{0:T(1024)S(1)} %multiply_add_fusion), kind=kOutput, calls=%fused_computation.4 | convolution fusion | flops 3836077056 | bytes 13274496 | tf_op jit(solution)/shard_map/dot_general | solution.py:17
  513.2 40.1 %all-to-all-done.4 = bf16[512,2,1728]{0,2,1:T(8,128)(2,1)S(1)} async-done(((bf16[512,2,1728]{0,2,1:T(8,128)(2,1)}), bf16[512,2,1728]{0,2,1:T(8,128)(2,1)S(1)}, u32[]{:S(2)}, u32[]{:S(2)}) %all-to-all-start.4) | async-done | bytes 3538976 | tf_op jit(solution)/shard_map/all_to_all | solution.py:79
  553.3 3.7 copy.23
  557.1 9.3 %convolution_multiply_fusion = f32[1728,864]{1,0:T(8,128)} fusion(bf16[1024,1728]{1,0:T(8,128)(2,1)} %bitcast.26, bf16[1024,864]{0,1:T(8,128)(2,1)} %all-gather.8.cloned.1.call-done), kind=kOutput, calls=%fused_computation.15 | convolution fusion | flops 3059140608 | bytes 11280384 | tf_op jit(solution)/shard_map/dot_general | solution.py:90
  (18 shorter events, 0.1 us)
Async XLA Ops:
  23.7 107.4 %all-to-all-start = ((bf16[16,54,2560]{2,1,0:T(8,128)(2,1)}), bf16[16,54,2560]{2,1,0:T(8,128)(2,1)}, u32[]{:S(2)}, u32[]{:S(2)}) async-start(bf16[16,54,2560]{2,1,0:T(8,128)(2,1)} %reshape.58), calls=%async_computation | async-start | bytes 9175040 | tf_op jit(solution)/shard_map/all_to_all | solution.py:55
  131.1 137.3 %all-to-all-start.1 = ((bf16[16,54,2560]{2,1,0:T(8,128)(2,1)}), bf16[16,54,2560]{2,1,0:T(8,128)(2,1)}, u32[]{:S(2)}, u32[]{:S(2)}) async-start(bf16[16,54,2560]{2,1,0:T(8,128)(2,1)} %reshape.60), calls=%async_computation.1 | async-start | bytes 9175040 | tf_op jit(solution)/shard_map/all_to_all | solution.py:55
  135.9 155.4 %all-gather.4.cloned.1.call-start = ((), (), s32[]{:S(2)}) async-start(), calls=%async_computation.6 | async-start | bytes 5570560 | tf_op jit(solution)/shard_map/all_gather | solution.py:30
  268.4 15.6 %slice-start = ((s8[4423680]{0:T(1024)(128)(4,1)}), s8[229376]{0:T(1024)(128)(4,1)S(1)}, s32[]{:S(2)}) async-start(s8[4423680]{0:T(1024)(128)(4,1)} %bitcast.29), calls=%async_computation.9 | async-start | bytes 458752
  273.7 10.3 %copy-start = (bf16[864,2560]{1,0:T(8,128)(2,1)S(1)}, bf16[864,2560]{1,0:T(8,128)(2,1)}, u32[]{:S(2)}) copy-start(bf16[864,2560]{1,0:T(8,128)(2,1)} %reshape.61) | copy-start | bytes 13271044
  273.7 10.3 %slice-start.1 = ((s8[4423680]{0:T(1024)(128)(4,1)}), s8[4194304]{0:T(1024)(128)(4,1)S(1)}, s32[]{:S(2)}) async-start(s8[4423680]{0:T(1024)(128)(4,1)} %bitcast.29), calls=%async_computation.10 | async-start | bytes 8388608
  284.0 7.3 %slice-start.2 = ((bf16[864,2560]{1,0:T(8,128)(2,1)}), bf16[216,2560]{1,0:T(8,128)(2,1)S(1)}, s32[]{:S(2)}) async-start(bf16[864,2560]{1,0:T(8,128)(2,1)} %param.9), calls=%async_computation.11 | async-start | bytes 2211840 | tf_op jit(solution)/shard_map/slice | solution.py:77
  284.0 7.2 %slice-start.3 = ((bf16[864,2560]{1,0:T(8,128)(2,1)}), bf16[216,2560]{1,0:T(8,128)(2,1)S(1)}, s32[]{:S(2)}) async-start(bf16[864,2560]{1,0:T(8,128)(2,1)} %param.10), calls=%async_computation.12 | async-start | bytes 2211840 | tf_op jit(solution)/shard_map/slice | solution.py:77
  297.2 19.8 %all-to-all-start.3 = ((bf16[2,512,432]{1,2,0:T(8,128)(2,1)}), bf16[2,512,432]{1,2,0:T(8,128)(2,1)S(1)}, u32[]{:S(2)}, u32[]{:S(2)}) async-start(bf16[2,512,432]{1,2,0:T(8,128)(2,1)} %bitcast.23), calls=%async_computation.3 | async-start | bytes 1769472 | tf_op jit(solution)/shard_map/all_to_all | solution.py:65
  317.0 1.0 copy-start.1
  318.0 44.3 %all-to-all-start.5 = ((bf16[2,512,1728]{1,2,0:T(8,128)(2,1)}), bf16[2,512,1728]{1,2,0:T(8,128)(2,1)S(1)}, u32[]{:S(2)}, u32[]{:S(2)}) async-start(bf16[2,512,1728]{1,2,0:T(8,128)(2,1)} %bitcast.25), calls=%async_computation.5 | async-start | bytes 7077888 | tf_op jit(solution)/shard_map/all_to_all | solution.py:65
  362.2 127.9 %all-to-all-start.2 = ((bf16[16,54,2560]{2,1,0:T(8,128)(2,1)}), bf16[16,54,2560]{2,1,0:T(8,128)(2,1)}, u32[]{:S(2)}, u32[]{:S(2)}) async-start(bf16[16,54,2560]{2,1,0:T(8,128)(2,1)} %reshape.62), calls=%async_computation.2 | async-start | bytes 9175040 | tf_op jit(solution)/shard_map/all_to_all | solution.py:55
  367.9 122.2 %all-gather.6.cloned.1.call-start = ((), (), s32[]{:S(2)}) async-start(), calls=%async_computation.7 | async-start | bytes 3760128 | tf_op jit(solution)/shard_map/all_gather | solution.py:78
  490.1 63.2 %all-to-all-start.4 = ((bf16[512,2,1728]{0,2,1:T(8,128)(2,1)}), bf16[512,2,1728]{0,2,1:T(8,128)(2,1)S(1)}, u32[]{:S(2)}, u32[]{:S(2)}) async-start(bf16[512,2,1728]{0,2,1:T(8,128)(2,1)} %bitcast.27), calls=%async_computation.4 | async-start | bytes 7077888 | tf_op jit(solution)/shard_map/all_to_all | solution.py:79
  494.1 62.9 %all-gather.8.cloned.1.call-start = ((), (), s32[]{:S(2)}) async-start(), calls=%async_computation.8 | async-start | bytes 2654208 | tf_op jit(solution)/shard_map/all_gather | solution.py:86
Sparse Core Ops, SparseCore 0:
  139.0 107.7 all-gather.3
  371.0 97.0 all-gather.5
  498.1 48.0 all-gather.7

commit v2 on v1

--- a/solution.py
+++ b/solution.py
@@ -21,14 +21,24 @@
     data_size = lax.axis_size("dp")
     model_size = lax.axis_size("mp")
     position = lax.axis_index("dp")
+    model_position = lax.axis_index("mp")
     unit_count = gate_first.shape[0]
-    feature_cols = gate_first.shape[1]
     capacity = -(-unit_count // data_size)
+    capacity = -(-capacity // 8) * 8
     slots = data_size * capacity
     factor = 1.0 / math.sqrt(D)
 
-    everyone = lax.all_gather(tokens, "dp", axis=0, tiled=True)
-    token_count = everyone.shape[0]
+    parities = [list(range(parity, data_size, 2)) for parity in range(2)]
+    swap = [(i, i ^ 1) for i in range(data_size)]
+    even = position % 2 == 0
+
+    def gather(block):
+        return lax.all_gather(block, "dp", axis=0, axis_index_groups=parities)
+
+    def both(mine, axis):
+        other = lax.ppermute(mine, "dp", swap)
+        halves = [jnp.where(even, mine, other), jnp.where(even, other, mine)]
+        return jnp.stack(halves, axis=axis)
 
     routing = matching.reshape(data_size, unit_count)
     owners = lax.div(routing, unit_count)
@@ -59,37 +69,53 @@
     def averaged(first, moved):
         return ((first.astype(jnp.float32) + moved.astype(jnp.float32)) * 0.5).astype(jnp.bfloat16)
 
-    def hidden(rows):
-        count = rows.shape[0] // 2
-        term = (matmul_t(everyone, rows) * factor).astype(jnp.bfloat16)
-        parts = lax.all_to_all(
-            term.reshape(model_size, -1, 2 * count), "mp", split_axis=0, concat_axis=0, tiled=True
-        )
-        pre = jnp.sum(parts.astype(jnp.float32), axis=0)
-        return (jax.nn.silu(pre[:, :count]) * pre[:, count:]).astype(jnp.bfloat16)
+    def shifted(value, by):
+        return lax.ppermute(value, "mp", [(i, (i + by) % model_size) for i in range(model_size)])
+
+    def shares(value, axis):
+        size = value.shape[axis] // model_size
+        out = []
+        for by in range(model_size):
+            target = (model_position + by) % model_size
+            part = lax.dynamic_slice_in_dim(value, target * size, size, axis)
+            out.append(part if by == 0 else shifted(part, by))
+        return out
+
+    def projected(rows):
+        term = (matmul_t(rows, everyone) * factor).astype(jnp.bfloat16)
+        return sum(part.astype(jnp.float32) for part in shares(term, 1))
+
+    def hidden(gate, up):
+        return (jax.nn.silu(gate) * up).astype(jnp.bfloat16)
 
     gate_out = pick(chooser, gate_second)
     up_out = pick(chooser, up_second)
+    down_out = pick(chooser, down_second)
+    mine, gate_out = lax.optimization_barrier((gather(tokens), gate_out))
     gate_in = exchange(gate_out)
+
+    everyone = both(mine, 0).reshape(-1, tokens.shape[1])
+    token_count = everyone.shape[0]
+    window = hidden(projected(gate_first[:CROWS]), projected(up_first[:CROWS]))
+    up_out, gate_in, window = lax.optimization_barrier((up_out, gate_in, window))
     up_in = exchange(up_out)
-    down_out = pick(chooser, down_second)
 
-    window = hidden(jnp.concatenate([gate_first[:CROWS], up_first[:CROWS]], axis=0))
-    window = lax.all_gather(window, "dp", axis=1, tiled=True)
-    window = lax.all_to_all(window, "mp", split_axis=1, concat_axis=0, tiled=True)
+    window = shares(both(gather(window), 1).reshape(data_size * CROWS, -1), 0)
+    gate_moved = pick(placer, gate_in)
+    gate_pre = projected(gate_moved)
+    down_out, up_in, gate_pre = lax.optimization_barrier((down_out, up_in, gate_pre))
+    down_in = exchange(down_out)
 
-    down_out, up_in, gate_in = lax.optimization_barrier((down_out, up_in, gate_in))
-    down_in = exchange(down_out)
-    gate_moved = pick(placer, gate_in)
+    up_in, window = lax.optimization_barrier((up_in, window))
     up_moved = pick(placer, up_in)
-    chosen = hidden(jnp.concatenate([gate_moved, up_moved], axis=0))
-    chosen = lax.all_gather(chosen, "mp", axis=0, tiled=True)
+    chosen = hidden(gate_pre, projected(up_moved))
+    correlation = matmul_t(window[0], chosen)
+    for by in range(1, model_size):
+        correlation = correlation + matmul_t(window[by], shifted(chosen, by))
+    correlation = correlation / math.sqrt(token_count)
     merged_gate = averaged(gate_first, gate_moved)
     merged_up = averaged(up_first, up_moved)
     merged_down = averaged(down_first, pick(placer, down_in))
-    correlation = lax.dot_general(
-        window, chosen, (((0,), (0,)), ((), ())), preferred_element_type=jnp.float32
-    ) / math.sqrt(token_count)
     return (merged_gate, merged_up, merged_down, correlation)
 
 

time: 575 us -> 442 us (0.77)
  waiting for transfers between devices: 396 us -> 302 us
  local copies, waits for them, and re-layouts: 40.7 us -> 1.53 us
    all_to_all x3, waiting for transfers between devices: 320 us -> 76.2 us  [exchange(): lax.all_to_all(rows.reshape(data_size, capacity, -1), 'dp', split_axis=0,...]
    all_gather x3 -> x2, waiting for transfers between devices: 0.01 us -> 130 us  [gather(): return lax.all_gather(block, 'dp', axis=0, axis_index_groups=parities)]
    ppermute x0 -> x8, waiting for transfers between devices: none -> 94.6 us  [the longest x6 89.6 us: shifted(): lax.ppermute(value, 'mp', [(i, (i + by) % model_size) for i in range(mode...]
    all_to_all x3 -> x0, waiting for transfers between devices: 75 us -> none  [the longest x1 40.1 us: local(): lax.all_to_all(window, 'mp', split_axis=1, concat_axis=0, tiled=True)]
    reshape x8 -> x0, local copies, waits for them, and re-layouts: 34.9 us -> none  [the longest x3 16 us: exchange(): return lax.all_to_all(rows.reshape(data_size, capacity, -1), 'dp', split_...]
    all_to_all x3 -> x0, starting transfers between devices: 11.8 us -> none  [the longest x2 7.79 us: hidden(): lax.all_to_all(term.reshape(model_size, -1, 2 * count), 'mp', split_axis=...]
    dot_general x1 -> x0, matrix products: 9.29 us -> none  [local(): lax.dot_general(window, chosen, (((0,), (0,)), ((), ())), preferred_eleme...]
    dot_general x2 -> x6, matrix products: 18.9 us -> 27.1 us  [matmul_t(): lax.dot_general(a, b, (((1,), (1,)), ((), ())), preferred_element_type=jn...]
  transfers between devices with their start and end apart: 9 -> 13, of which waited for: 5 -> 9; matrix products, arithmetic and copies ran while one was open for 18% -> 18% of each run, Pallas kernels for 0% -> 0%
where the time goes in v2:
time: 442 us; the launch traced here: 437 us
  waiting for transfers between devices  302 us (68%)
  matrix products  78.5 us (18%)
  starting transfers between devices  31.6 us (7%)
  between operations  14.3 us (3%)
  other arithmetic  9.51 us (2%)
    all_gather x2, waiting for transfers between devices, gather(): return lax.all_gather(block, 'dp', axis=0, axis_index_groups=parities)  130 us
    ppermute x6, waiting for transfers between devices, shifted(): lax.ppermute(value, 'mp', [(i, (i + by) % model_size) for i in range(mode...  89.6 us
    all_to_all x3, waiting for transfers between devices, exchange(): lax.all_to_all(rows.reshape(data_size, capacity, -1), 'dp', split_axis=0,...  76.2 us
    dot_general x6, matrix products, pick(): jnp.dot(onehot, rows, preferred_element_type=jnp.float32)  51.1 us
    dot_general x6, matrix products, matmul_t(): lax.dot_general(a, b, (((1,), (1,)), ((), ())), preferred_element_type=jn...  27.1 us
    all_to_all x3, starting transfers between devices, exchange(): lax.all_to_all(rows.reshape(data_size, capacity, -1), 'dp', split_axis=0,...  23.5 us
  transfers between devices with their start and end apart: 13, of which 9 were waited for; matrix products, arithmetic and copies ran while one was open for 18% of the time, Pallas kernels for 0%

profile of v2, /device:TPU:13, one launch (start us, length us, event | category | flops | bytes accessed | tf_op | source)
XLA Modules:
  0.0 437.5 jit_solution(4641278320615705097)
XLA Ops:
  7.2 0.7 all-gather.5.cloned.1.call-update
  7.9 0.9 reshape.54
  8.9 0.3 fusion.11
  9.2 0.9 select_reduce_fusion
  10.2 9.0 %convolution_convert_fusion.1 = bf16[896,2560]{1,0:T(8,128)(2,1)} fusion(bf16[864,2560]{1,0:T(8,128)(2,1)} %param.12, s32[896]{0:T(1024)S(1)} %eq.90), kind=kOutput, calls=%fused_computation.5 | convolution fusion | flops 3966685184 | bytes 9014784 | tf_op jit(solution)/shard_map/dot_general | solution.py:17
  19.1 44.5 %all-gather.5.cloned.1.call-done = bf16[512,2560]{1,0:T(8,128)(2,1)} async-done(((bf16[64,2560]{1,0:T(8,128)(2,1)}), bf16[512,2560]{1,0:T(8,128)(2,1)}) %all-gather.5.cloned.1.call-update) | async-done | bytes 2621456 | tf_op jit(solution)/shard_map/all_gather | solution.py:36
  63.6 7.5 %all-to-all-start = ((bf16[16,56,2560]{2,1,0:T(8,128)(2,1)}), bf16[16,56,2560]{2,1,0:T(8,128)(2,1)}, u32[]{:S(2)}, u32[]{:S(2)}) async-start(bf16[16,56,2560]{2,1,0:T(8,128)(2,1)} %bitcast.58), calls=%async_computation | async-start | bytes 9175040 | tf_op jit(solution)/shard_map/all_to_all | solution.py:65
  71.1 0.5 collective-permute-start
  71.6 5.1 %collective-permute-done = bf16[8,64,2560]{2,1,0:T(8,128)(2,1)} collective-permute-done((bf16[8,64,2560]{2,1,0:T(8,128)(2,1)S(1)}, bf16[8,64,2560]{2,1,0:T(8,128)(2,1)}, u32[]{:S(2)}, u32[]{:S(2)}) %collective-permute-start) | collective-permute-done | bytes 2621472 | tf_op jit(solution)/shard_map/ppermute | solution.py:39
  76.7 2.1 select_bitcast_fusion.1
  78.8 0.5 pad_maximum_fusion
  79.3 3.8 fusion.10
  83.1 1.2 collective-permute-start.2
  84.4 3.0 fusion.9
  87.4 0.5 collective-permute-start.1
  87.9 6.7 %convolution_convert_fusion.2 = bf16[896,2560]{1,0:T(8,128)(2,1)} fusion(bf16[864,2560]{1,0:T(8,128)(2,1)S(1)} %bitcast.66, s32[896]{0:T(1024)S(1)} %eq.90), kind=kOutput, calls=%fused_computation.6 | convolution fusion | flops 3966685184 | bytes 9014784 | tf_op jit(solution)/shard_map/dot_general | solution.py:17
  94.6 0.4 collective-permute-done.1
  95.0 0.9 fusion.15
  95.9 76.2 %all-to-all-done = bf16[16,56,2560]{2,1,0:T(8,128)(2,1)} async-done(((bf16[16,56,2560]{2,1,0:T(8,128)(2,1)}), bf16[16,56,2560]{2,1,0:T(8,128)(2,1)}, u32[]{:S(2)}, u32[]{:S(2)}) %all-to-all-start) | async-done | bytes 4587552 | tf_op jit(solution)/shard_map/all_to_all | solution.py:65
  172.0 4.8 %all-to-all-start.1 = ((bf16[16,56,2560]{2,1,0:T(8,128)(2,1)}), bf16[16,56,2560]{2,1,0:T(8,128)(2,1)}, u32[]{:S(2)}, u32[]{:S(2)}) async-start(bf16[16,56,2560]{2,1,0:T(8,128)(2,1)} %bitcast.59), calls=%async_computation.1 | async-start | bytes 9175040 | tf_op jit(solution)/shard_map/all_to_all | solution.py:65
  177.0 0.5 all-gather.7.cloned.1.call-update
  177.6 0.8 dynamic-slice_divide_fusion
  178.3 0.4 convert_reduce_fusion
  178.8 0.8 multiply_add_fusion
  179.6 10.2 %multiply_convert_fusion.2 = (bf16[864,2560]{1,0:T(8,128)(2,1)}, bf16[864,2560]{1,0:T(8,128)(2,1)}) fusion(bf16[864,2560]{1,0:T(8,128)(2,1)} %param.9, bf16[896,2560]{1,0:T(8,128)(2,1)} %bitcast.2, s32[864]{0:T(1024)S(1)} %multiply_add_fusion), kind=kOutput, calls=%fused_computation.2 | convolution fusion | flops 3977662464 | bytes 17862016 | tf_op jit(solution)/shard_map/dot_general | solution.py:17
  189.8 85.6 %all-gather.7.cloned.1.call-done = bf16[1728,512]{1,0:T(8,128)(2,1)} async-done(((bf16[216,512]{1,0:T(8,128)(2,1)}), bf16[1728,512]{1,0:T(8,128)(2,1)}) %all-gather.7.cloned.1.call-update) | async-done | bytes 1769488 | tf_op jit(solution)/shard_map/all_gather | solution.py:36
  275.3 0.7 collective-permute-start.4
  276.0 8.7 %multiply_convert_fusion.4 = bf16[864,1024]{1,0:T(8,128)(2,1)S(1)} fusion(bf16[864,2560]{1,0:T(8,128)(2,1)} %get-tuple-element.33, bf16[1024,2560]{1,0:T(8,128)(2,1)} %bitcast.54), kind=kOutput, calls=%fused_computation.13 | convolution fusion | flops 4531617792 | bytes 11436032 | tf_op jit(solution)/shard_map/dot_general | solution.py:13
  284.8 1.3 collective-permute-start.3
  286.1 6.7 %convolution_convert_fusion = bf16[896,2560]{1,0:T(8,128)(2,1)} fusion(bf16[864,2560]{1,0:T(8,128)(2,1)S(1)} %bitcast.68, s32[896]{0:T(1024)S(1)} %eq.90), kind=kOutput, calls=%fused_computation.4 | convolution fusion | flops 3966685184 | bytes 9014784 | tf_op jit(solution)/shard_map/dot_general | solution.py:17
  292.8 13.3 %collective-permute-done.3 = bf16[864,512]{1,0:T(8,128)(2,1)S(1)} collective-permute-done((bf16[864,512]{1,0:T(8,128)(2,1)S(1)}, bf16[864,512]{1,0:T(8,128)(2,1)S(1)}, u32[]{:S(2)}, u32[]{:S(2)}) %collective-permute-start.3) | collective-permute-done | bytes 884768 | tf_op jit(solution)/shard_map/ppermute | solution.py:73
  306.1 0.3 convert_add_fusion
  306.4 11.3 %all-to-all-start.2 = ((bf16[16,56,2560]{2,1,0:T(8,128)(2,1)}), bf16[16,56,2560]{2,1,0:T(8,128)(2,1)}, u32[]{:S(2)}, u32[]{:S(2)}) async-start(bf16[16,56,2560]{2,1,0:T(8,128)(2,1)} %bitcast.60), calls=%async_computation.2 | async-start | bytes 9175040 | tf_op jit(solution)/shard_map/all_to_all | solution.py:65
  317.7 1.9 select_bitcast_fusion.3
  319.6 0.3 pad_maximum_fusion.1
  319.9 0.2 constant_dynamic-slice_fusion
  320.2 1.3 collective-permute-start.5
  321.4 38.7 %collective-permute-done.5 = bf16[1728,512]{1,0:T(8,128)(2,1)S(1)} collective-permute-done((bf16[1728,512]{1,0:T(8,128)(2,1)S(1)}, bf16[1728,512]{1,0:T(8,128)(2,1)S(1)}, u32[]{:S(2)}, u32[]{:S(2)}) %collective-permute-start.5) | collective-permute-done | bytes 1769504 | tf_op jit(solution)/shard_map/ppermute | solution.py:73
  360.1 9.0 %multiply_convert_fusion.1 = (bf16[864,2560]{1,0:T(8,128)(2,1)}, bf16[864,2560]{1,0:T(8,128)(2,1)S(1)}) fusion(bf16[864,2560]{1,0:T(8,128)(2,1)S(1)} %bitcast.70, bf16[896,2560]{1,0:T(8,128)(2,1)} %bitcast.11, s32[864]{0:T(1024)S(1)} %multiply_add_fusion), kind=kOutput, calls=%fused_computation.1 | convolution fusion | flops 3977662464 | bytes 17862016 | tf_op jit(solution)/shard_map/dot_general | solution.py:17
  369.2 4.8 %multiply_convert_fusion.3 = bf16[864,1024]{1,0:T(8,128)(2,1)S(1)} fusion(bf16[864,2560]{1,0:T(8,128)(2,1)S(1)} %get-tuple-element.35, bf16[1024,2560]{1,0:T(8,128)(2,1)S(1)} %bitcast.57), kind=kOutput, calls=%fused_computation.12 | convolution fusion | flops 4531617792 | bytes 11436032 | tf_op jit(solution)/shard_map/dot_general | solution.py:13
  374.0 1.2 collective-permute-start.6
  375.3 19.0 %collective-permute-done.6 = bf16[864,512]{1,0:T(8,128)(2,1)S(1)} collective-permute-done((bf16[864,512]{1,0:T(8,128)(2,1)S(1)}, bf16[864,512]{1,0:T(8,128)(2,1)S(1)}, u32[]{:S(2)}, u32[]{:S(2)}) %collective-permute-start.6) | collective-permute-done | bytes 884768 | tf_op jit(solution)/shard_map/ppermute | solution.py:73
  394.2 0.6 multiply_convert_fusion.5
  394.9 1.2 collective-permute-start.7
  396.1 18.3 %collective-permute-done.7 = bf16[864,512]{1,0:T(8,128)(2,1)S(1)} collective-permute-done((bf16[864,512]{1,0:T(8,128)(2,1)S(1)}, bf16[864,512]{1,0:T(8,128)(2,1)S(1)}, u32[]{:S(2)}, u32[]{:S(2)}) %collective-permute-start.7) | collective-permute-done | bytes 884768 | tf_op jit(solution)/shard_map/ppermute | solution.py:73
  414.3 2.0 fusion.16
  416.4 4.8 %add_multiply_fusion = f32[1728,864]{1,0:T(8,128)} fusion(f32[1728,864]{1,0:T(8,128)S(1)} %fusion.16, bf16[1728,512]{1,0:T(8,128)(2,1)S(1)} %get-tuple-element.23, bf16[864,512]{1,0:T(8,128)(2,1)S(1)} %multiply_convert_fusion.5), kind=kOutput, calls=%fused_computation.3 | convolution fusion | flops 1531809792 | bytes 14598144 | tf_op jit(solution)/shard_map/dot_general | solution.py:13
  421.2 9.4 %multiply_convert_fusion = bf16[864,2560]{1,0:T(8,128)(2,1)} fusion(bf16[864,2560]{1,0:T(8,128)(2,1)} %param.11, bf16[896,2560]{1,0:T(8,128)(2,1)} %bitcast.18, s32[864]{0:T(1024)S(1)} %multiply_add_fusion), kind=kOutput, calls=%fused_computation | convolution fusion | flops 3977662464 | bytes 13438336 | tf_op jit(solution)/shard_map/dot_general | solution.py:17
  (39 shorter events, 0.7 us)
Async XLA Ops:
  7.2 56.5 %all-gather.5.cloned.1.call-start = ((), (), s32[]{:S(2)}) async-start(), calls=%async_computation.3 | async-start | bytes 2949120 | tf_op jit(solution)/shard_map/all_gather | solution.py:36
  63.6 7.5 %copy-start.1 = (bf16[512,2560]{1,0:T(8,128)(2,1)S(1)}, bf16[512,2560]{1,0:T(8,128)(2,1)}, u32[]{:S(2)}) copy-start(bf16[512,2560]{1,0:T(8,128)(2,1)} %all-gather.5.cloned.1.call-done) | copy-start | bytes 7864324
  63.6 108.4 %all-to-all-start = ((bf16[16,56,2560]{2,1,0:T(8,128)(2,1)}), bf16[16,56,2560]{2,1,0:T(8,128)(2,1)}, u32[]{:S(2)}, u32[]{:S(2)}) async-start(bf16[16,56,2560]{2,1,0:T(8,128)(2,1)} %bitcast.58), calls=%async_computation | async-start | bytes 9175040 | tf_op jit(solution)/shard_map/all_to_all | solution.py:65
  71.1 5.5 %collective-permute-start = (bf16[8,64,2560]{2,1,0:T(8,128)(2,1)S(1)}, bf16[8,64,2560]{2,1,0:T(8,128)(2,1)}, u32[]{:S(2)}, u32[]{:S(2)}) collective-permute-start(bf16[8,64,2560]{2,1,0:T(8,128)(2,1)S(1)} %bitcast.61), channel_id=1, source_target_pairs={{0,2},{2,0},{4,6},{6,4},{8,10},{10,8},{12,14},{14,12},{16,18},{18,... | collective-permute-start | bytes 7864328 | tf_op jit(solution)/shard_map/ppermute | solution.py:39
  79.2 5.1 %copy-start = (bf16[2,8,64,2560]{3,2,1,0:T(8,128)(2,1)}, bf16[2,8,64,2560]{3,2,1,0:T(8,128)(2,1)S(1)}, u32[]{:S(2)}) copy-start(bf16[2,8,64,2560]{3,2,1,0:T(8,128)(2,1)S(1)} %pad_maximum_fusion) | copy-start | bytes 15728644
  83.0 4.9 %slice-start.2 = ((s8[4423680]{0:T(1024)(128)(4,1)}), s8[4194304]{0:T(1024)(128)(4,1)S(1)}, s32[]{:S(2)}) async-start(s8[4423680]{0:T(1024)(128)(4,1)} %bitcast.65), calls=%async_computation.7 | async-start | bytes 8388608
  83.1 4.8 %slice-start.3 = ((s8[4423680]{0:T(1024)(128)(4,1)}), s8[229376]{0:T(1024)(128)(4,1)S(1)}, s32[]{:S(2)}) async-start(s8[4423680]{0:T(1024)(128)(4,1)} %bitcast.65), calls=%async_computation.8 | async-start | bytes 458752
  83.1 11.5 %collective-permute-start.2 = (bf16[216,512]{1,0:T(8,128)(2,1)S(1)}, bf16[216,512]{1,0:T(8,128)(2,1)S(1)}, u32[]{:S(2)}, u32[]{:S(2)}) collective-permute-start(bf16[216,512]{1,0:T(8,128)(2,1)S(1)} %dynamic-slice_bitcast_fusion), channel_id=1, source_target_pairs={{0,1},{1,0},{2,3},{3,2},{4,5},{5,4},{6,7},{7,6},{8,9},{9,8},{10,11... | collective-permute-start | bytes 663560 | tf_op jit(solution)/shard_map/ppermute | solution.py:73
  87.4 7.6 %collective-permute-start.1 = (bf16[216,512]{1,0:T(8,128)(2,1)S(1)}, bf16[216,512]{1,0:T(8,128)(2,1)S(1)}, u32[]{:S(2)}, u32[]{:S(2)}) collective-permute-start(bf16[216,512]{1,0:T(8,128)(2,1)S(1)} %dynamic-slice_bitcast_fusion.1), channel_id=1, source_target_pairs={{0,1},{1,0},{2,3},{3,2},{4,5},{5,4},{6,7},{7,6},{8,9},{9,8},{10,11... | collective-permute-start | bytes 663560 | tf_op jit(solution)/shard_map/ppermute | solution.py:73
  172.0 134.4 %all-to-all-start.1 = ((bf16[16,56,2560]{2,1,0:T(8,128)(2,1)}), bf16[16,56,2560]{2,1,0:T(8,128)(2,1)}, u32[]{:S(2)}, u32[]{:S(2)}) async-start(bf16[16,56,2560]{2,1,0:T(8,128)(2,1)} %bitcast.59), calls=%async_computation.1 | async-start | bytes 9175040 | tf_op jit(solution)/shard_map/all_to_all | solution.py:65
  176.8 98.5 %all-gather.7.cloned.1.call-start = ((), (), s32[]{:S(2)}) async-start(), calls=%async_computation.4 | async-start | bytes 1990656 | tf_op jit(solution)/shard_map/all_gather | solution.py:36
  179.6 106.5 %slice-start.4 = ((s8[4423680]{0:T(1024)(128)(4,1)}), s8[229376]{0:T(1024)(128)(4,1)S(1)}, s32[]{:S(2)}) async-start(s8[4423680]{0:T(1024)(128)(4,1)} %bitcast.67), calls=%async_computation.9 | async-start | bytes 458752
  275.3 42.3 %collective-permute-start.4 = (bf16[8,216,512]{2,1,0:T(8,128)(2,1)}, bf16[8,216,512]{2,1,0:T(8,128)(2,1)}, u32[]{:S(2)}, u32[]{:S(2)}) collective-permute-start(bf16[8,216,512]{2,1,0:T(8,128)(2,1)} %bitcast.63), channel_id=1, source_target_pairs={{0,2},{2,0},{4,6},{6,4},{8,10},{10,8},{12,14},{14,12},{16,18},{18,... | collective-permute-start | bytes 5308424 | tf_op jit(solution)/shard_map/ppermute | solution.py:39
  276.0 10.1 %slice-start.5 = ((s8[4423680]{0:T(1024)(128)(4,1)}), s8[4194304]{0:T(1024)(128)(4,1)S(1)}, s32[]{:S(2)}) async-start(s8[4423680]{0:T(1024)(128)(4,1)} %bitcast.67), calls=%async_computation.10 | async-start | bytes 8388608
  284.8 21.3 %collective-permute-start.3 = (bf16[864,512]{1,0:T(8,128)(2,1)S(1)}, bf16[864,512]{1,0:T(8,128)(2,1)S(1)}, u32[]{:S(2)}, u32[]{:S(2)}) collective-permute-start(bf16[864,512]{1,0:T(8,128)(2,1)S(1)} %constant_dynamic-slice_fusion.2), channel_id=1, source_target_pairs={{0,1},{1,0},{2,3},{3,2},{4,5},{5,4},{6,7},{7,6},{8,9},{9,8},{10,11... | collective-permute-start | bytes 2654216 | tf_op jit(solution)/shard_map/ppermute | solution.py:73
  306.4 11.3 %copy-start.2 = (bf16[1728,512]{1,0:T(8,128)(2,1)S(1)}, bf16[1728,512]{1,0:T(8,128)(2,1)}, u32[]{:S(2)}) copy-start(bf16[1728,512]{1,0:T(8,128)(2,1)} %all-gather.7.cloned.1.call-done) | copy-start | bytes 5308420
  306.4 114.8 %all-to-all-start.2 = ((bf16[16,56,2560]{2,1,0:T(8,128)(2,1)}), bf16[16,56,2560]{2,1,0:T(8,128)(2,1)}, u32[]{:S(2)}, u32[]{:S(2)}) async-start(bf16[16,56,2560]{2,1,0:T(8,128)(2,1)} %bitcast.60), calls=%async_computation.2 | async-start | bytes 9175040 | tf_op jit(solution)/shard_map/all_to_all | solution.py:65
  317.7 42.4 %slice-start.6 = ((s8[4423680]{0:T(1024)(128)(4,1)}), s8[4194304]{0:T(1024)(128)(4,1)S(1)}, s32[]{:S(2)}) async-start(s8[4423680]{0:T(1024)(128)(4,1)} %bitcast.69), calls=%async_computation.11 | async-start | bytes 8388608
  319.6 40.6 %slice-start.7 = ((s8[4423680]{0:T(1024)(128)(4,1)}), s8[229376]{0:T(1024)(128)(4,1)S(1)}, s32[]{:S(2)}) async-start(s8[4423680]{0:T(1024)(128)(4,1)} %bitcast.69), calls=%async_computation.12 | async-start | bytes 458752
  319.9 49.2 %slice-start = ((s8[5242880]{0:T(1024)(128)(4,1)}), s8[1048576]{0:T(1024)(128)(4,1)S(1)}, s32[]{:S(2)}) async-start(s8[5242880]{0:T(1024)(128)(4,1)} %bitcast.55), calls=%async_computation.5 | async-start | bytes 2097152
  320.2 39.9 %collective-permute-start.5 = (bf16[1728,512]{1,0:T(8,128)(2,1)S(1)}, bf16[1728,512]{1,0:T(8,128)(2,1)S(1)}, u32[]{:S(2)}, u32[]{:S(2)}) collective-permute-start(bf16[1728,512]{1,0:T(8,128)(2,1)S(1)} %get-tuple-element.28), channel_id=1, source_target_pairs={{0,1},{1,0},{2,3},{3,2},{4,5},{5,4},{6,7},{7,6},{8,9},{9,8},{10,11... | collective-permute-start | bytes 5308424 | tf_op jit(solution)/shard_map/ppermute | solution.py:73
  360.1 9.0 %slice-start.1 = ((s8[5242880]{0:T(1024)(128)(4,1)}), s8[4194304]{0:T(1024)(128)(4,1)S(1)}, s32[]{:S(2)}) async-start(s8[5242880]{0:T(1024)(128)(4,1)} %bitcast.55), calls=%async_computation.6 | async-start | bytes 8388608
  374.0 20.2 %collective-permute-start.6 = (bf16[864,512]{1,0:T(8,128)(2,1)S(1)}, bf16[864,512]{1,0:T(8,128)(2,1)S(1)}, u32[]{:S(2)}, u32[]{:S(2)}) collective-permute-start(bf16[864,512]{1,0:T(8,128)(2,1)S(1)} %constant_dynamic-slice_fusion.3), channel_id=1, source_target_pairs={{0,1},{1,0},{2,3},{3,2},{4,5},{5,4},{6,7},{7,6},{8,9},{9,8},{10,11... | collective-permute-start | bytes 2654216 | tf_op jit(solution)/shard_map/ppermute | solution.py:73
  394.9 19.5 %collective-permute-start.7 = (bf16[864,512]{1,0:T(8,128)(2,1)S(1)}, bf16[864,512]{1,0:T(8,128)(2,1)S(1)}, u32[]{:S(2)}, u32[]{:S(2)}) collective-permute-start(bf16[864,512]{1,0:T(8,128)(2,1)S(1)} %multiply_convert_fusion.5), channel_id=1, source_target_pairs={{0,1},{1,0},{2,3},{3,2},{4,5},{5,4},{6,7},{7,6},{8,9},{9,8},{10,11... | collective-permute-start | bytes 2654216 | tf_op jit(solution)/shard_map/ppermute | solution.py:73
Sparse Core Ops, SparseCore 0:
  10.2 53.4 all-gather.4
  180.4 94.9 all-gather.6

commit v3 on v2

--- a/solution.py
+++ b/solution.py
@@ -4,6 +4,7 @@
 import jax.numpy as jnp
 from jax import lax
 from jax.sharding import PartitionSpec as P
+
 
 D = 5120
 CROWS = 216
@@ -91,7 +92,7 @@
     gate_out = pick(chooser, gate_second)
     up_out = pick(chooser, up_second)
     down_out = pick(chooser, down_second)
-    mine, gate_out = lax.optimization_barrier((gather(tokens), gate_out))
+    mine = gather(tokens)
     gate_in = exchange(gate_out)
 
     everyone = both(mine, 0).reshape(-1, tokens.shape[1])
@@ -100,13 +101,15 @@
     up_out, gate_in, window = lax.optimization_barrier((up_out, gate_in, window))
     up_in = exchange(up_out)
 
-    window = shares(both(gather(window), 1).reshape(data_size * CROWS, -1), 0)
+    window = gather(window)
     gate_moved = pick(placer, gate_in)
     gate_pre = projected(gate_moved)
-    down_out, up_in, gate_pre = lax.optimization_barrier((down_out, up_in, gate_pre))
+    down_out, up_in, gate_pre, window = lax.optimization_barrier(
+        (down_out, up_in, gate_pre, window)
+    )
     down_in = exchange(down_out)
 
-    up_in, window = lax.optimization_barrier((up_in, window))
+    window = shares(both(window, 1).reshape(data_size * CROWS, -1), 0)
     up_moved = pick(placer, up_in)
     chosen = hidden(gate_pre, projected(up_moved))
     correlation = matmul_t(window[0], chosen)

time: 442 us -> 406 us (0.919)
  waiting for transfers between devices: 302 us -> 276 us
  starting transfers between devices: 31.6 us -> 23.8 us
    all_to_all x3, waiting for transfers between devices: 76.2 us -> 30.2 us  [exchange(): lax.all_to_all(rows.reshape(data_size, capacity, -1), 'dp', split_axis=0,...]
    all_gather x2, waiting for transfers between devices: 130 us -> 156 us  [gather(): return lax.all_gather(block, 'dp', axis=0, axis_index_groups=parities)]
    all_to_all x3, starting transfers between devices: 23.5 us -> 16.4 us  [exchange(): lax.all_to_all(rows.reshape(data_size, capacity, -1), 'dp', split_axis=0,...]
    ppermute x6, waiting for transfers between devices: 89.6 us -> 85 us  [shifted(): lax.ppermute(value, 'mp', [(i, (i + by) % model_size) for i in range(mode...]
  transfers between devices with their start and end apart: 13 -> 13, of which waited for: 9 -> 9; matrix products, arithmetic and copies ran while one was open for 18% -> 20% of each run, Pallas kernels for 0% -> 0%
where the time goes in v3:
time: 406 us; the launch traced here: 404 us
  waiting for transfers between devices  276 us (68%)
  matrix products  77.5 us (19%)
  starting transfers between devices  23.8 us (6%)
  between operations  14.3 us (4%)
  other arithmetic  9.96 us (2%)
    all_gather x2, waiting for transfers between devices, gather(): return lax.all_gather(block, 'dp', axis=0, axis_index_groups=parities)  156 us
    ppermute x6, waiting for transfers between devices, shifted(): lax.ppermute(value, 'mp', [(i, (i + by) % model_size) for i in range(mode...  85 us
    dot_general x6, matrix products, pick(): jnp.dot(onehot, rows, preferred_element_type=jnp.float32)  51.3 us
    all_to_all x3, waiting for transfers between devices, exchange(): lax.all_to_all(rows.reshape(data_size, capacity, -1), 'dp', split_axis=0,...  30.2 us
    dot_general x6, matrix products, matmul_t(): lax.dot_general(a, b, (((1,), (1,)), ((), ())), preferred_element_type=jn...  25.9 us
    all_to_all x3, starting transfers between devices, exchange(): lax.all_to_all(rows.reshape(data_size, capacity, -1), 'dp', split_axis=0,...  16.4 us
  transfers between devices with their start and end apart: 13, of which 9 were waited for; matrix products, arithmetic and copies ran while one was open for 20% of the time, Pallas kernels for 0%

profile of v3, /device:TPU:13, one launch (start us, length us, event | category | flops | bytes accessed | tf_op | source)
XLA Modules:
  0.0 404.3 jit_solution(7254344327825449882)
XLA Ops:
  7.2 0.7 all-gather.5.cloned.1.call-update
  7.9 0.9 reshape.54
  8.9 0.3 fusion.12
  9.2 0.9 select_reduce_fusion
  10.2 9.0 %convolution_convert_fusion.1 = bf16[896,2560]{1,0:T(8,128)(2,1)} fusion(bf16[864,2560]{1,0:T(8,128)(2,1)} %param.12, s32[896]{0:T(1024)S(1)} %eq.90), kind=kOutput, calls=%fused_computation.5 | convolution fusion | flops 3966685184 | bytes 9014784 | tf_op jit(solution)/shard_map/dot_general | solution.py:18
  19.1 6.5 %all-to-all-start = ((bf16[16,56,2560]{2,1,0:T(8,128)(2,1)}), bf16[16,56,2560]{2,1,0:T(8,128)(2,1)}, u32[]{:S(2)}, u32[]{:S(2)}) async-start(bf16[16,56,2560]{2,1,0:T(8,128)(2,1)} %bitcast.60), calls=%async_computation | async-start | bytes 9175040 | tf_op jit(solution)/shard_map/all_to_all | solution.py:66
  25.7 96.3 %all-gather.5.cloned.1.call-done = bf16[512,2560]{1,0:T(8,128)(2,1)} async-done(((bf16[64,2560]{1,0:T(8,128)(2,1)}), bf16[512,2560]{1,0:T(8,128)(2,1)}) %all-gather.5.cloned.1.call-update) | async-done | bytes 2621456 | tf_op jit(solution)/shard_map/all_gather | solution.py:37
  122.0 0.9 collective-permute-start
  122.8 4.7 %collective-permute-done = bf16[8,64,2560]{2,1,0:T(8,128)(2,1)S(1)} collective-permute-done((bf16[8,64,2560]{2,1,0:T(8,128)(2,1)}, bf16[8,64,2560]{2,1,0:T(8,128)(2,1)S(1)}, u32[]{:S(2)}, u32[]{:S(2)}) %collective-permute-start) | collective-permute-done | bytes 2621472 | tf_op jit(solution)/shard_map/ppermute | solution.py:40
  127.6 2.1 select_bitcast_fusion.1
  129.7 0.5 pad_maximum_fusion
  130.2 3.8 fusion.10
  134.0 1.3 collective-permute-start.1
  135.3 3.0 fusion.11
  138.3 0.5 collective-permute-start.2
  138.8 6.7 %convolution_convert_fusion.2 = bf16[896,2560]{1,0:T(8,128)(2,1)} fusion(bf16[864,2560]{1,0:T(8,128)(2,1)S(1)} %bitcast.68, s32[896]{0:T(1024)S(1)} %eq.90), kind=kOutput, calls=%fused_computation.6 | convolution fusion | flops 3966685184 | bytes 9014784 | tf_op jit(solution)/shard_map/dot_general | solution.py:18
  145.7 0.9 fusion.16
  146.5 6.5 %all-to-all-done = bf16[16,56,2560]{2,1,0:T(8,128)(2,1)} async-done(((bf16[16,56,2560]{2,1,0:T(8,128)(2,1)}), bf16[16,56,2560]{2,1,0:T(8,128)(2,1)}, u32[]{:S(2)}, u32[]{:S(2)}) %all-to-all-start) | async-done | bytes 4587552 | tf_op jit(solution)/shard_map/all_to_all | solution.py:66
  153.1 4.9 %all-to-all-start.1 = ((bf16[16,56,2560]{2,1,0:T(8,128)(2,1)}), bf16[16,56,2560]{2,1,0:T(8,128)(2,1)}, u32[]{:S(2)}, u32[]{:S(2)}) async-start(bf16[16,56,2560]{2,1,0:T(8,128)(2,1)} %bitcast.61), calls=%async_computation.1 | async-start | bytes 9175040 | tf_op jit(solution)/shard_map/all_to_all | solution.py:66
  158.0 0.2 all-gather.7.cloned.1.call-start
  158.2 0.8 dynamic-slice_divide_fusion
  159.0 0.4 convert_reduce_fusion
  159.4 0.8 multiply_add_fusion
  160.3 9.6 %multiply_convert_fusion.2 = (bf16[864,2560]{1,0:T(8,128)(2,1)}, bf16[864,2560]{1,0:T(8,128)(2,1)S(1)}) fusion(bf16[864,2560]{1,0:T(8,128)(2,1)} %param.9, bf16[896,2560]{1,0:T(8,128)(2,1)} %bitcast.1, s32[864]{0:T(1024)S(1)} %multiply_add_fusion), kind=kOutput, calls=%fused_computation.2 | convolution fusion | flops 3977662464 | bytes 17862016 | tf_op jit(solution)/shard_map/dot_general | solution.py:18
  169.9 4.8 %multiply_convert_fusion.4 = bf16[864,1024]{1,0:T(8,128)(2,1)S(1)} fusion(bf16[864,2560]{1,0:T(8,128)(2,1)S(1)} %get-tuple-element.23, bf16[1024,2560]{1,0:T(8,128)(2,1)S(1)} %bitcast.56), kind=kOutput, calls=%fused_computation.13 | convolution fusion | flops 4531617792 | bytes 11436032 | tf_op jit(solution)/shard_map/dot_general | solution.py:14
  174.7 0.1 constant_dynamic-slice_fusion.1
  174.8 1.3 collective-permute-start.3
  176.1 6.9 %convolution_convert_fusion = bf16[896,2560]{1,0:T(8,128)(2,1)} fusion(bf16[864,2560]{1,0:T(8,128)(2,1)S(1)} %bitcast.70, s32[896]{0:T(1024)S(1)} %eq.90), kind=kOutput, calls=%fused_computation.4 | convolution fusion | flops 3966685184 | bytes 9014784 | tf_op jit(solution)/shard_map/dot_general | solution.py:18
  182.9 12.8 %collective-permute-done.3 = bf16[864,512]{1,0:T(8,128)(2,1)S(1)} collective-permute-done((bf16[864,512]{1,0:T(8,128)(2,1)S(1)}, bf16[864,512]{1,0:T(8,128)(2,1)S(1)}, u32[]{:S(2)}, u32[]{:S(2)}) %collective-permute-start.3) | collective-permute-done | bytes 884768 | tf_op jit(solution)/shard_map/ppermute | solution.py:74
  195.8 1.5 convert_add_fusion
  197.3 59.3 %all-gather.7.cloned.1.call-done = bf16[1728,512]{1,0:T(8,128)(2,1)} async-done(((bf16[216,512]{1,0:T(8,128)(2,1)}), bf16[1728,512]{1,0:T(8,128)(2,1)}) %all-gather.7.cloned.1.call-update) | async-done | bytes 1769488 | tf_op jit(solution)/shard_map/all_gather | solution.py:37
  256.5 23.7 %all-to-all-done.1 = bf16[16,56,2560]{2,1,0:T(8,128)(2,1)} async-done(((bf16[16,56,2560]{2,1,0:T(8,128)(2,1)}), bf16[16,56,2560]{2,1,0:T(8,128)(2,1)}, u32[]{:S(2)}, u32[]{:S(2)}) %all-to-all-start.1) | async-done | bytes 4587552 | tf_op jit(solution)/shard_map/all_to_all | solution.py:66
  280.2 4.9 %all-to-all-start.2 = ((bf16[16,56,2560]{2,1,0:T(8,128)(2,1)}), bf16[16,56,2560]{2,1,0:T(8,128)(2,1)}, u32[]{:S(2)}, u32[]{:S(2)}) async-start(bf16[16,56,2560]{2,1,0:T(8,128)(2,1)} %bitcast.62), calls=%async_computation.2 | async-start | bytes 9175040 | tf_op jit(solution)/shard_map/all_to_all | solution.py:66
  285.2 0.5 collective-permute-start.4
  285.6 9.7 %multiply_convert_fusion.1 = (bf16[864,2560]{1,0:T(8,128)(2,1)}, bf16[864,2560]{1,0:T(8,128)(2,1)S(1)}) fusion(bf16[864,2560]{1,0:T(8,128)(2,1)} %param.10, bf16[896,2560]{1,0:T(8,128)(2,1)} %bitcast.11, s32[864]{0:T(1024)S(1)} %multiply_add_fusion), kind=kOutput, calls=%fused_computation.1 | convolution fusion | flops 3977662464 | bytes 17862016 | tf_op jit(solution)/shard_map/dot_general | solution.py:18
  295.3 4.8 %multiply_convert_fusion.3 = bf16[864,1024]{1,0:T(8,128)(2,1)S(1)} fusion(bf16[864,2560]{1,0:T(8,128)(2,1)S(1)} %get-tuple-element.25, bf16[1024,2560]{1,0:T(8,128)(2,1)S(1)} %bitcast.59), kind=kOutput, calls=%fused_computation.12 | convolution fusion | flops 4531617792 | bytes 11436032 | tf_op jit(solution)/shard_map/dot_general | solution.py:14
  300.2 1.3 collective-permute-start.5
  301.5 0.2 select_bitcast_fusion.3
  301.7 0.3 pad_maximum_fusion.1
  302.1 1.3 constant_dynamic-slice_fusion.2
  303.4 0.2 collective-permute-start.6
  303.6 17.8 %collective-permute-done.5 = bf16[864,512]{1,0:T(8,128)(2,1)S(1)} collective-permute-done((bf16[864,512]{1,0:T(8,128)(2,1)S(1)}, bf16[864,512]{1,0:T(8,128)(2,1)S(1)}, u32[]{:S(2)}, u32[]{:S(2)}) %collective-permute-start.5) | collective-permute-done | bytes 884768 | tf_op jit(solution)/shard_map/ppermute | solution.py:74
  321.4 1.5 multiply_convert_fusion.5
  322.9 1.2 collective-permute-start.7
  324.2 54.2 %collective-permute-done.7 = bf16[864,512]{1,0:T(8,128)(2,1)} collective-permute-done((bf16[864,512]{1,0:T(8,128)(2,1)}, bf16[864,512]{1,0:T(8,128)(2,1)}, u32[]{:S(2)}, u32[]{:S(2)}) %collective-permute-start.7) | collective-permute-done | bytes 884768 | tf_op jit(solution)/shard_map/ppermute | solution.py:74
  378.4 3.7 fusion.18
  382.1 5.9 %add_multiply_fusion = f32[1728,864]{1,0:T(8,128)} fusion(f32[1728,864]{1,0:T(8,128)S(1)} %fusion.18, bf16[864,512]{1,0:T(8,128)(2,1)} %multiply_convert_fusion.5, bf16[3456,512]{1,0:T(8,128)(2,1)S(1)} %bitcast.51, s32[]{:T(128)S(6)} %select_n.93), kind=kOutput, calls=%fused_computation.3 | convolution fusion | flops 1531809792 | bytes 14819332 | tf_op jit(solution)/shard_map/dot_general | solution.py:14
  388.0 9.4 %multiply_convert_fusion = bf16[864,2560]{1,0:T(8,128)(2,1)} fusion(bf16[864,2560]{1,0:T(8,128)(2,1)} %param.11, bf16[896,2560]{1,0:T(8,128)(2,1)} %bitcast.14, s32[864]{0:T(1024)S(1)} %multiply_add_fusion), kind=kOutput, calls=%fused_computation | convolution fusion | flops 3977662464 | bytes 13438336 | tf_op jit(solution)/shard_map/dot_general | solution.py:18
  (39 shorter events, 0.5 us)
Async XLA Ops:
  7.2 114.8 %all-gather.5.cloned.1.call-start = ((), (), s32[]{:S(2)}) async-start(), calls=%async_computation.3 | async-start | bytes 2949120 | tf_op jit(solution)/shard_map/all_gather | solution.py:37
  19.1 133.9 %all-to-all-start = ((bf16[16,56,2560]{2,1,0:T(8,128)(2,1)}), bf16[16,56,2560]{2,1,0:T(8,128)(2,1)}, u32[]{:S(2)}, u32[]{:S(2)}) async-start(bf16[16,56,2560]{2,1,0:T(8,128)(2,1)} %bitcast.60), calls=%async_computation | async-start | bytes 9175040 | tf_op jit(solution)/shard_map/all_to_all | solution.py:66
  122.0 5.6 %collective-permute-start = (bf16[8,64,2560]{2,1,0:T(8,128)(2,1)}, bf16[8,64,2560]{2,1,0:T(8,128)(2,1)S(1)}, u32[]{:S(2)}, u32[]{:S(2)}) collective-permute-start(bf16[8,64,2560]{2,1,0:T(8,128)(2,1)} %bitcast.63), channel_id=1, source_target_pairs={{0,2},{2,0},{4,6},{6,4},{8,10},{10,8},{12,14},{14,12},{16,18},{18,... | collective-permute-start | bytes 7864328 | tf_op jit(solution)/shard_map/ppermute | solution.py:40
  130.2 5.1 %copy-start.1 = (bf16[2,8,64,2560]{3,2,1,0:T(8,128)(2,1)}, bf16[2,8,64,2560]{3,2,1,0:T(8,128)(2,1)S(1)}, u32[]{:S(2)}) copy-start(bf16[2,8,64,2560]{3,2,1,0:T(8,128)(2,1)S(1)} %pad_maximum_fusion) | copy-start | bytes 15728644
  134.0 4.8 %slice-start.4 = ((s8[4423680]{0:T(1024)(128)(4,1)}), s8[4194304]{0:T(1024)(128)(4,1)S(1)}, s32[]{:S(2)}) async-start(s8[4423680]{0:T(1024)(128)(4,1)} %bitcast.67), calls=%async_computation.9 | async-start | bytes 8388608
  134.0 4.8 %slice-start.5 = ((s8[4423680]{0:T(1024)(128)(4,1)}), s8[229376]{0:T(1024)(128)(4,1)S(1)}, s32[]{:S(2)}) async-start(s8[4423680]{0:T(1024)(128)(4,1)} %bitcast.67), calls=%async_computation.10 | async-start | bytes 458752
  134.0 11.5 %collective-permute-start.1 = (bf16[216,512]{1,0:T(8,128)(2,1)S(1)}, bf16[216,512]{1,0:T(8,128)(2,1)S(1)}, u32[]{:S(2)}, u32[]{:S(2)}) collective-permute-start(bf16[216,512]{1,0:T(8,128)(2,1)S(1)} %dynamic-slice_bitcast_fusion.1), channel_id=1, source_target_pairs={{0,1},{1,0},{2,3},{3,2},{4,5},{5,4},{6,7},{7,6},{8,9},{9,8},{10,11... | collective-permute-start | bytes 663560 | tf_op jit(solution)/shard_map/ppermute | solution.py:74
  138.3 7.4 %collective-permute-start.2 = (bf16[216,512]{1,0:T(8,128)(2,1)S(1)}, bf16[216,512]{1,0:T(8,128)(2,1)S(1)}, u32[]{:S(2)}, u32[]{:S(2)}) collective-permute-start(bf16[216,512]{1,0:T(8,128)(2,1)S(1)} %dynamic-slice_bitcast_fusion), channel_id=1, source_target_pairs={{0,1},{1,0},{2,3},{3,2},{4,5},{5,4},{6,7},{7,6},{8,9},{9,8},{10,11... | collective-permute-start | bytes 663560 | tf_op jit(solution)/shard_map/ppermute | solution.py:74
  153.0 16.8 %slice-start = ((s8[5242880]{0:T(1024)(128)(4,1)}), s8[1048576]{0:T(1024)(128)(4,1)S(1)}, s32[]{:S(2)}) async-start(s8[5242880]{0:T(1024)(128)(4,1)} %bitcast.54), calls=%async_computation.5 | async-start | bytes 2097152
  153.1 127.2 %all-to-all-start.1 = ((bf16[16,56,2560]{2,1,0:T(8,128)(2,1)}), bf16[16,56,2560]{2,1,0:T(8,128)(2,1)}, u32[]{:S(2)}, u32[]{:S(2)}) async-start(bf16[16,56,2560]{2,1,0:T(8,128)(2,1)} %bitcast.61), calls=%async_computation.1 | async-start | bytes 9175040 | tf_op jit(solution)/shard_map/all_to_all | solution.py:66
  158.0 98.5 %all-gather.7.cloned.1.call-start = ((), (), s32[]{:S(2)}) async-start(), calls=%async_computation.4 | async-start | bytes 1990656 | tf_op jit(solution)/shard_map/all_gather | solution.py:37
  160.3 9.6 %slice-start.1 = ((s8[5242880]{0:T(1024)(128)(4,1)}), s8[4194304]{0:T(1024)(128)(4,1)S(1)}, s32[]{:S(2)}) async-start(s8[5242880]{0:T(1024)(128)(4,1)} %bitcast.54), calls=%async_computation.6 | async-start | bytes 8388608
  160.3 15.8 %slice-start.6 = ((s8[4423680]{0:T(1024)(128)(4,1)}), s8[4194304]{0:T(1024)(128)(4,1)S(1)}, s32[]{:S(2)}) async-start(s8[4423680]{0:T(1024)(128)(4,1)} %bitcast.69), calls=%async_computation.11 | async-start | bytes 8388608
  169.9 6.2 %slice-start.7 = ((s8[4423680]{0:T(1024)(128)(4,1)}), s8[229376]{0:T(1024)(128)(4,1)S(1)}, s32[]{:S(2)}) async-start(s8[4423680]{0:T(1024)(128)(4,1)} %bitcast.69), calls=%async_computation.12 | async-start | bytes 458752
  174.8 21.0 %collective-permute-start.3 = (bf16[864,512]{1,0:T(8,128)(2,1)S(1)}, bf16[864,512]{1,0:T(8,128)(2,1)S(1)}, u32[]{:S(2)}, u32[]{:S(2)}) collective-permute-start(bf16[864,512]{1,0:T(8,128)(2,1)S(1)} %constant_dynamic-slice_fusion.1), channel_id=1, source_target_pairs={{0,1},{1,0},{2,3},{3,2},{4,5},{5,4},{6,7},{7,6},{8,9},{9,8},{10,11... | collective-permute-start | bytes 2654216 | tf_op jit(solution)/shard_map/ppermute | solution.py:74
  280.2 4.9 %copy-start.2 = (bf16[1728,512]{1,0:T(8,128)(2,1)S(1)}, bf16[1728,512]{1,0:T(8,128)(2,1)}, u32[]{:S(2)}) copy-start(bf16[1728,512]{1,0:T(8,128)(2,1)} %all-gather.7.cloned.1.call-done) | copy-start | bytes 5308420
  280.2 107.8 %all-to-all-start.2 = ((bf16[16,56,2560]{2,1,0:T(8,128)(2,1)}), bf16[16,56,2560]{2,1,0:T(8,128)(2,1)}, u32[]{:S(2)}, u32[]{:S(2)}) async-start(bf16[16,56,2560]{2,1,0:T(8,128)(2,1)} %bitcast.62), calls=%async_computation.2 | async-start | bytes 9175040 | tf_op jit(solution)/shard_map/all_to_all | solution.py:66
  285.1 10.2 %slice-start.2 = ((s8[5242880]{0:T(1024)(128)(4,1)}), s8[1048576]{0:T(1024)(128)(4,1)S(1)}, s32[]{:S(2)}) async-start(s8[5242880]{0:T(1024)(128)(4,1)} %bitcast.57), calls=%async_computation.7 | async-start | bytes 2097152
  285.2 10.2 %slice-start.3 = ((s8[5242880]{0:T(1024)(128)(4,1)}), s8[4194304]{0:T(1024)(128)(4,1)S(1)}, s32[]{:S(2)}) async-start(s8[5242880]{0:T(1024)(128)(4,1)} %bitcast.57), calls=%async_computation.8 | async-start | bytes 8388608
  285.2 16.3 %collective-permute-start.4 = (bf16[8,216,512]{2,1,0:T(8,128)(2,1)S(1)}, bf16[8,216,512]{2,1,0:T(8,128)(2,1)S(1)}, u32[]{:S(2)}, u32[]{:S(2)}) collective-permute-start(bf16[8,216,512]{2,1,0:T(8,128)(2,1)S(1)} %bitcast.65), channel_id=1, source_target_pairs={{0,2},{2,0},{4,6},{6,4},{8,10},{10,8},{12,14},{14,12},{16,18},{18,... | collective-permute-start | bytes 5308424 | tf_op jit(solution)/shard_map/ppermute | solution.py:40
  300.2 21.2 %collective-permute-start.5 = (bf16[864,512]{1,0:T(8,128)(2,1)S(1)}, bf16[864,512]{1,0:T(8,128)(2,1)S(1)}, u32[]{:S(2)}, u32[]{:S(2)}) collective-permute-start(bf16[864,512]{1,0:T(8,128)(2,1)S(1)} %constant_dynamic-slice_fusion), channel_id=1, source_target_pairs={{0,1},{1,0},{2,3},{3,2},{4,5},{5,4},{6,7},{7,6},{8,9},{9,8},{10,11... | collective-permute-start | bytes 2654216 | tf_op jit(solution)/shard_map/ppermute | solution.py:74
  301.7 19.7 %copy-start = (f32[864,512]{1,0:T(8,128)S(1)}, f32[864,512]{1,0:T(8,128)}, u32[]{:S(2)}) copy-start(f32[864,512]{1,0:T(8,128)} %convert_add_fusion) | copy-start | bytes 5308420
  303.4 75.0 %collective-permute-start.6 = (bf16[1728,512]{1,0:T(8,128)(2,1)}, bf16[1728,512]{1,0:T(8,128)(2,1)}, u32[]{:S(2)}, u32[]{:S(2)}) collective-permute-start(bf16[1728,512]{1,0:T(8,128)(2,1)} %constant_dynamic-slice_fusion.2), channel_id=1, source_target_pairs={{0,1},{1,0},{2,3},{3,2},{4,5},{5,4},{6,7},{7,6},{8,9},{9,8},{10,11... | collective-permute-start | bytes 5308424 | tf_op jit(solution)/shard_map/ppermute | solution.py:74
  322.9 55.5 %collective-permute-start.7 = (bf16[864,512]{1,0:T(8,128)(2,1)}, bf16[864,512]{1,0:T(8,128)(2,1)}, u32[]{:S(2)}, u32[]{:S(2)}) collective-permute-start(bf16[864,512]{1,0:T(8,128)(2,1)} %multiply_convert_fusion.5), channel_id=1, source_target_pairs={{0,1},{1,0},{2,3},{3,2},{4,5},{5,4},{6,7},{7,6},{8,9},{9,8},{10,11... | collective-permute-start | bytes 2654216 | tf_op jit(solution)/shard_map/ppermute | solution.py:74
Sparse Core Ops, SparseCore 0:
  10.2 111.7 all-gather.4
  161.6 94.9 all-gather.6

commit v4 on v3

--- a/solution.py
+++ b/solution.py
@@ -4,7 +4,6 @@
 import jax.numpy as jnp
 from jax import lax
 from jax.sharding import PartitionSpec as P
-
 
 D = 5120
 CROWS = 216
@@ -30,11 +29,10 @@
     factor = 1.0 / math.sqrt(D)
 
     parities = [list(range(parity, data_size, 2)) for parity in range(2)]
+    lanes = [list(range(lane, data_size, 4)) for lane in range(4)]
+    pairs = [[i, i + 2] for i in range(data_size) if i % 4 < 2]
     swap = [(i, i ^ 1) for i in range(data_size)]
     even = position % 2 == 0
-
-    def gather(block):
-        return lax.all_gather(block, "dp", axis=0, axis_index_groups=parities)
 
     def both(mine, axis):
         other = lax.ppermute(mine, "dp", swap)
@@ -92,8 +90,10 @@
     gate_out = pick(chooser, gate_second)
     up_out = pick(chooser, up_second)
     down_out = pick(chooser, down_second)
-    mine = gather(tokens)
+    mine = lax.all_gather(tokens, "dp", axis=0, axis_index_groups=lanes)
+    mine, gate_out = lax.optimization_barrier((mine, gate_out))
     gate_in = exchange(gate_out)
+    mine = lax.all_gather(mine, "dp", axis=0, axis_index_groups=pairs)
 
     everyone = both(mine, 0).reshape(-1, tokens.shape[1])
     token_count = everyone.shape[0]
@@ -101,15 +101,17 @@
     up_out, gate_in, window = lax.optimization_barrier((up_out, gate_in, window))
     up_in = exchange(up_out)
 
-    window = gather(window)
+    window = lax.all_gather(window, "dp", axis=0, axis_index_groups=parities)
     gate_moved = pick(placer, gate_in)
     gate_pre = projected(gate_moved)
+    gate_pre, window = lax.optimization_barrier((gate_pre, window))
+    window = both(window, 1)
     down_out, up_in, gate_pre, window = lax.optimization_barrier(
         (down_out, up_in, gate_pre, window)
     )
     down_in = exchange(down_out)
 
-    window = shares(both(window, 1).reshape(data_size * CROWS, -1), 0)
+    window = shares(window.reshape(data_size * CROWS, -1), 0)
     up_moved = pick(placer, up_in)
     chosen = hidden(gate_pre, projected(up_moved))
     correlation = matmul_t(window[0], chosen)

time: 406 us -> 407 us (level)
  waiting for transfers between devices: 276 us -> 269 us
  matrix products: 77.5 us -> 81.9 us
    all_to_all x3, waiting for transfers between devices: 30.2 us -> 23.5 us  [exchange(): lax.all_to_all(rows.reshape(data_size, capacity, -1), 'dp', split_axis=0,...]
    all_gather x2 -> x3, waiting for transfers between devices: 156 us -> 149 us  [the longest x1 66.8 us: local(): mine = lax.all_gather(mine, 'dp', axis=0, axis_index_groups=pairs)]
    ppermute x6, waiting for transfers between devices: 85 us -> 90.9 us  [shifted(): lax.ppermute(value, 'mp', [(i, (i + by) % model_size) for i in range(mode...]
  transfers between devices with their start and end apart: 13 -> 14, of which waited for: 9 -> 11; matrix products, arithmetic and copies ran while one was open for 20% -> 22% of each run, Pallas kernels for 0% -> 0%
where the time goes in v4:
time: 407 us; the launch traced here: 404 us
  waiting for transfers between devices  269 us (66%)
  matrix products  81.9 us (20%)
  starting transfers between devices  23 us (6%)
  between operations  13.9 us (3%)
  other arithmetic  11.4 us (3%)
  local copies, waits for them, and re-layouts  4.73 us (1%)
    ppermute x6, waiting for transfers between devices, shifted(): lax.ppermute(value, 'mp', [(i, (i + by) % model_size) for i in range(mode...  90.9 us
    all_gather x1, waiting for transfers between devices, local(): mine = lax.all_gather(mine, 'dp', axis=0, axis_index_groups=pairs)  66.8 us
    all_gather x1, waiting for transfers between devices, local(): window = lax.all_gather(window, 'dp', axis=0, axis_index_groups=parities)  59.3 us
    dot_general x6, matrix products, pick(): jnp.dot(onehot, rows, preferred_element_type=jnp.float32)  53.2 us
    dot_general x6, matrix products, matmul_t(): lax.dot_general(a, b, (((1,), (1,)), ((), ())), preferred_element_type=jn...  28.4 us
    all_to_all x3, waiting for transfers between devices, exchange(): lax.all_to_all(rows.reshape(data_size, capacity, -1), 'dp', split_axis=0,...  23.5 us
    all_gather x1, waiting for transfers between devices, local(): mine = lax.all_gather(tokens, 'dp', axis=0, axis_index_groups=lanes)  23.1 us
    all_to_all x3, starting transfers between devices, exchange(): lax.all_to_all(rows.reshape(data_size, capacity, -1), 'dp', split_axis=0,...  15.8 us
  transfers between devices with their start and end apart: 14, of which 11 were waited for; matrix products, arithmetic and copies ran while one was open for 22% of the time, Pallas kernels for 0%

profile of v4, /device:TPU:13, one launch (start us, length us, event | category | flops | bytes accessed | tf_op | source)
XLA Modules:
  0.0 403.9 jit_solution(6946124877264658427)
XLA Ops:
  7.2 0.7 all-gather.7.cloned.1.call-update
  8.0 0.9 reshape.54
  9.2 0.9 select_reduce_fusion
  10.2 9.0 %convolution_convert_fusion.1 = bf16[896,2560]{1,0:T(8,128)(2,1)} fusion(bf16[864,2560]{1,0:T(8,128)(2,1)} %param.12, s32[896]{0:T(1024)S(1)} %eq.90), kind=kOutput, calls=%fused_computation.5 | convolution fusion | flops 3966685184 | bytes 9014784 | tf_op jit(solution)/shard_map/dot_general | solution.py:17
  19.2 23.1 %all-gather.7.cloned.1.call-done = bf16[256,2560]{1,0:T(8,128)(2,1)} async-done(((bf16[64,2560]{1,0:T(8,128)(2,1)}), bf16[256,2560]{1,0:T(8,128)(2,1)}) %all-gather.7.cloned.1.call-update) | async-done | bytes 1310736 | tf_op jit(solution)/shard_map/all_gather | solution.py:93
  42.3 6.1 %all-to-all-start = ((bf16[16,56,2560]{2,1,0:T(8,128)(2,1)}), bf16[16,56,2560]{2,1,0:T(8,128)(2,1)}, u32[]{:S(2)}, u32[]{:S(2)}) async-start(bf16[16,56,2560]{2,1,0:T(8,128)(2,1)} %bitcast.59), calls=%async_computation | async-start | bytes 9175040 | tf_op jit(solution)/shard_map/all_to_all | solution.py:64
  48.5 66.8 %all-gather.9.cloned.1.call-done = bf16[8,64,2560]{2,1,0:T(8,128)(2,1)} async-done(((bf16[4,64,2560]{2,1,0:T(8,128)(2,1)}), bf16[8,64,2560]{2,1,0:T(8,128)(2,1)}) %all-gather.9.cloned.1.call-update) | async-done | bytes 2621456 | tf_op jit(solution)/shard_map/all_gather | solution.py:96
  115.2 0.6 collective-permute-start
  115.8 4.7 %collective-permute-done = bf16[2,4,64,2560]{3,2,1,0:T(8,128)(2,1)S(1)} collective-permute-done((bf16[2,4,64,2560]{3,2,1,0:T(8,128)(2,1)}, bf16[2,4,64,2560]{3,2,1,0:T(8,128)(2,1)S(1)}, u32[]{:S(2)}, u32[]{:S(2)}) %collective-permute-start) | collective-permute-done | bytes 2621472 | tf_op jit(solution)/shard_map/ppermute | solution.py:38
  120.5 2.1 select_bitcast_fusion.1
  122.6 0.5 pad_maximum_fusion
  123.1 3.8 fusion.10
  126.9 1.3 collective-permute-start.1
  128.2 3.0 fusion.11
  131.2 0.5 collective-permute-start.2
  131.7 6.7 %convolution_convert_fusion.2 = bf16[896,2560]{1,0:T(8,128)(2,1)} fusion(bf16[864,2560]{1,0:T(8,128)(2,1)S(1)} %bitcast.68, s32[896]{0:T(1024)S(1)} %eq.90), kind=kOutput, calls=%fused_computation.6 | convolution fusion | flops 3966685184 | bytes 9014784 | tf_op jit(solution)/shard_map/dot_general | solution.py:17
  138.6 0.9 fusion.16
  139.4 10.0 %all-to-all-done = bf16[16,56,2560]{2,1,0:T(8,128)(2,1)} async-done(((bf16[16,56,2560]{2,1,0:T(8,128)(2,1)}), bf16[16,56,2560]{2,1,0:T(8,128)(2,1)}, u32[]{:S(2)}, u32[]{:S(2)}) %all-to-all-start) | async-done | bytes 4587552 | tf_op jit(solution)/shard_map/all_to_all | solution.py:64
  149.5 4.9 %all-to-all-start.1 = ((bf16[16,56,2560]{2,1,0:T(8,128)(2,1)}), bf16[16,56,2560]{2,1,0:T(8,128)(2,1)}, u32[]{:S(2)}, u32[]{:S(2)}) async-start(bf16[16,56,2560]{2,1,0:T(8,128)(2,1)} %bitcast.60), calls=%async_computation.1 | async-start | bytes 9175040 | tf_op jit(solution)/shard_map/all_to_all | solution.py:64
  154.6 0.8 dynamic-slice_divide_fusion
  155.3 0.4 convert_reduce_fusion
  155.8 0.8 multiply_add_fusion
  156.6 9.6 %multiply_convert_fusion.2 = (bf16[864,2560]{1,0:T(8,128)(2,1)}, bf16[864,2560]{1,0:T(8,128)(2,1)S(1)}) fusion(bf16[864,2560]{1,0:T(8,128)(2,1)} %param.9, bf16[896,2560]{1,0:T(8,128)(2,1)} %bitcast.2, s32[864]{0:T(1024)S(1)} %multiply_add_fusion), kind=kOutput, calls=%fused_computation.2 | convolution fusion | flops 3977662464 | bytes 17862016 | tf_op jit(solution)/shard_map/dot_general | solution.py:17
  166.2 4.8 %multiply_convert_fusion.4 = bf16[864,1024]{1,0:T(8,128)(2,1)S(1)} fusion(bf16[864,2560]{1,0:T(8,128)(2,1)S(1)} %get-tuple-element.31, bf16[1024,2560]{1,0:T(8,128)(2,1)S(1)} %bitcast.58), kind=kOutput, calls=%fused_computation.13 | convolution fusion | flops 4531617792 | bytes 11436032 | tf_op jit(solution)/shard_map/dot_general | solution.py:13
  171.1 1.2 collective-permute-start.3
  172.3 19.7 %collective-permute-done.3 = bf16[864,512]{1,0:T(8,128)(2,1)S(1)} collective-permute-done((bf16[864,512]{1,0:T(8,128)(2,1)S(1)}, bf16[864,512]{1,0:T(8,128)(2,1)S(1)}, u32[]{:S(2)}, u32[]{:S(2)}) %collective-permute-start.3) | collective-permute-done | bytes 884768 | tf_op jit(solution)/shard_map/ppermute | solution.py:72
  192.1 1.5 convert_add_fusion
  193.6 59.3 %all-gather.11.cloned.1.call-done = bf16[1728,512]{1,0:T(8,128)(2,1)} async-done(((bf16[216,512]{1,0:T(8,128)(2,1)}), bf16[1728,512]{1,0:T(8,128)(2,1)}) %all-gather.11.cloned.1.call-update) | async-done | bytes 1769488 | tf_op jit(solution)/shard_map/all_gather | solution.py:104
  252.9 0.7 collective-permute-start.4
  253.5 9.0 %convolution_convert_fusion = bf16[896,2560]{1,0:T(8,128)(2,1)} fusion(bf16[864,2560]{1,0:T(8,128)(2,1)} %param.14, s32[896]{0:T(1024)S(1)} %eq.90), kind=kOutput, calls=%fused_computation.4 | convolution fusion | flops 3966685184 | bytes 9014784 | tf_op jit(solution)/shard_map/dot_general | solution.py:17
  262.7 0.3 pad_maximum_fusion.1
  263.1 13.5 %all-to-all-done.1 = bf16[16,56,2560]{2,1,0:T(8,128)(2,1)} async-done(((bf16[16,56,2560]{2,1,0:T(8,128)(2,1)}), bf16[16,56,2560]{2,1,0:T(8,128)(2,1)}, u32[]{:S(2)}, u32[]{:S(2)}) %all-to-all-start.1) | async-done | bytes 4587552 | tf_op jit(solution)/shard_map/all_to_all | solution.py:64
  276.6 4.8 %all-to-all-start.2 = ((bf16[16,56,2560]{2,1,0:T(8,128)(2,1)}), bf16[16,56,2560]{2,1,0:T(8,128)(2,1)}, u32[]{:S(2)}, u32[]{:S(2)}) async-start(bf16[16,56,2560]{2,1,0:T(8,128)(2,1)} %bitcast.61), calls=%async_computation.2 | async-start | bytes 9175040 | tf_op jit(solution)/shard_map/all_to_all | solution.py:64
  281.3 9.5 %multiply_convert_fusion.1 = (bf16[864,2560]{1,0:T(8,128)(2,1)}, bf16[864,2560]{1,0:T(8,128)(2,1)S(1)}) fusion(bf16[864,2560]{1,0:T(8,128)(2,1)} %param.10, bf16[896,2560]{1,0:T(8,128)(2,1)} %bitcast.12, s32[864]{0:T(1024)S(1)} %multiply_add_fusion), kind=kOutput, calls=%fused_computation.1 | convolution fusion | flops 3977662464 | bytes 17862016 | tf_op jit(solution)/shard_map/dot_general | solution.py:17
  290.8 7.2 %multiply_convert_fusion.3 = bf16[864,1024]{1,0:T(8,128)(2,1)S(1)} fusion(bf16[864,2560]{1,0:T(8,128)(2,1)S(1)} %get-tuple-element.33, bf16[1024,2560]{1,0:T(8,128)(2,1)} %bitcast.55), kind=kOutput, calls=%fused_computation.12 | convolution fusion | flops 4531617792 | bytes 11436032 | tf_op jit(solution)/shard_map/dot_general | solution.py:13
  298.1 1.2 copy-done.3
  299.3 1.0 constant_dynamic-slice_fusion
  300.3 1.2 collective-permute-start.5
  301.5 1.3 constant_dynamic-slice_fusion.2
  302.8 0.3 collective-permute-start.6
  303.1 18.3 %collective-permute-done.5 = bf16[864,512]{1,0:T(8,128)(2,1)} collective-permute-done((bf16[864,512]{1,0:T(8,128)(2,1)}, bf16[864,512]{1,0:T(8,128)(2,1)}, u32[]{:S(2)}, u32[]{:S(2)}) %collective-permute-start.5) | collective-permute-done | bytes 884768 | tf_op jit(solution)/shard_map/ppermute | solution.py:72
  321.4 2.9 multiply_convert_fusion.5
  324.4 1.2 collective-permute-start.7
  325.6 33.8 %collective-permute-done.6 = bf16[1728,512]{1,0:T(8,128)(2,1)} collective-permute-done((bf16[1728,512]{1,0:T(8,128)(2,1)}, bf16[1728,512]{1,0:T(8,128)(2,1)}, u32[]{:S(2)}, u32[]{:S(2)}) %collective-permute-start.6) | collective-permute-done | bytes 1769504 | tf_op jit(solution)/shard_map/ppermute | solution.py:72
  359.3 19.0 %collective-permute-done.7 = bf16[864,512]{1,0:T(8,128)(2,1)} collective-permute-done((bf16[864,512]{1,0:T(8,128)(2,1)}, bf16[864,512]{1,0:T(8,128)(2,1)}, u32[]{:S(2)}, u32[]{:S(2)}) %collective-permute-start.7) | collective-permute-done | bytes 884768 | tf_op jit(solution)/shard_map/ppermute | solution.py:72
  378.3 3.7 fusion.18
  382.0 5.9 %add_multiply_fusion = f32[1728,864]{1,0:T(8,128)} fusion(f32[1728,864]{1,0:T(8,128)S(1)} %fusion.18, bf16[864,512]{1,0:T(8,128)(2,1)} %multiply_convert_fusion.5, bf16[3456,512]{1,0:T(8,128)(2,1)S(1)} %bitcast.52, s32[]{:T(128)S(6)} %select_n.93), kind=kOutput, calls=%fused_computation.3 | convolution fusion | flops 1531809792 | bytes 14819332 | tf_op jit(solution)/shard_map/dot_general | solution.py:13
  387.9 9.4 %multiply_convert_fusion = bf16[864,2560]{1,0:T(8,128)(2,1)} fusion(bf16[864,2560]{1,0:T(8,128)(2,1)} %param.11, bf16[896,2560]{1,0:T(8,128)(2,1)} %bitcast.18, s32[864]{0:T(1024)S(1)} %multiply_add_fusion), kind=kOutput, calls=%fused_computation | convolution fusion | flops 3977662464 | bytes 13438336 | tf_op jit(solution)/shard_map/dot_general | solution.py:17
  (34 shorter events, 1.3 us)
Async XLA Ops:
  7.2 35.1 %all-gather.7.cloned.1.call-start = ((), (), s32[]{:S(2)}) async-start(), calls=%async_computation.3 | async-start | bytes 1638400 | tf_op jit(solution)/shard_map/all_gather | solution.py:93
  7.9 107.3 %all-gather.9.cloned.1.call-start = ((), (), s32[]{:S(2)}) async-start(), calls=%async_computation.4 | async-start | bytes 3932160 | tf_op jit(solution)/shard_map/all_gather | solution.py:96
  42.3 107.1 %all-to-all-start = ((bf16[16,56,2560]{2,1,0:T(8,128)(2,1)}), bf16[16,56,2560]{2,1,0:T(8,128)(2,1)}, u32[]{:S(2)}, u32[]{:S(2)}) async-start(bf16[16,56,2560]{2,1,0:T(8,128)(2,1)} %bitcast.59), calls=%async_computation | async-start | bytes 9175040 | tf_op jit(solution)/shard_map/all_to_all | solution.py:64
  115.2 5.3 %collective-permute-start = (bf16[2,4,64,2560]{3,2,1,0:T(8,128)(2,1)}, bf16[2,4,64,2560]{3,2,1,0:T(8,128)(2,1)S(1)}, u32[]{:S(2)}, u32[]{:S(2)}) collective-permute-start(bf16[2,4,64,2560]{3,2,1,0:T(8,128)(2,1)} %bitcast.62), channel_id=1, source_target_pairs={{0,2},{2,0},{4,6},{6,4},{8,10},{10,8},{12,14},{14,12},{16,18},{18,... | collective-permute-start | bytes 7864328 | tf_op jit(solution)/shard_map/ppermute | solution.py:38
  123.1 5.1 %copy-start.1 = (bf16[2,2,4,64,2560]{4,3,2,1,0:T(8,128)(2,1)}, bf16[2,2,4,64,2560]{4,3,2,1,0:T(8,128)(2,1)S(1)}, u32[]{:S(2)}) copy-start(bf16[2,2,4,64,2560]{4,3,2,1,0:T(8,128)(2,1)S(1)} %pad_maximum_fusion) | copy-start | bytes 15728644
  126.9 4.8 %slice-start.2 = ((s8[4423680]{0:T(1024)(128)(4,1)}), s8[4194304]{0:T(1024)(128)(4,1)S(1)}, s32[]{:S(2)}) async-start(s8[4423680]{0:T(1024)(128)(4,1)} %bitcast.67), calls=%async_computation.8 | async-start | bytes 8388608
  126.9 4.8 %slice-start.3 = ((s8[4423680]{0:T(1024)(128)(4,1)}), s8[229376]{0:T(1024)(128)(4,1)S(1)}, s32[]{:S(2)}) async-start(s8[4423680]{0:T(1024)(128)(4,1)} %bitcast.67), calls=%async_computation.9 | async-start | bytes 458752
  126.9 11.5 %collective-permute-start.1 = (bf16[216,512]{1,0:T(8,128)(2,1)S(1)}, bf16[216,512]{1,0:T(8,128)(2,1)S(1)}, u32[]{:S(2)}, u32[]{:S(2)}) collective-permute-start(bf16[216,512]{1,0:T(8,128)(2,1)S(1)} %dynamic-slice_bitcast_fusion.1), channel_id=1, source_target_pairs={{0,1},{1,0},{2,3},{3,2},{4,5},{5,4},{6,7},{7,6},{8,9},{9,8},{10,11... | collective-permute-start | bytes 663560 | tf_op jit(solution)/shard_map/ppermute | solution.py:72
  131.2 7.3 %collective-permute-start.2 = (bf16[216,512]{1,0:T(8,128)(2,1)S(1)}, bf16[216,512]{1,0:T(8,128)(2,1)S(1)}, u32[]{:S(2)}, u32[]{:S(2)}) collective-permute-start(bf16[216,512]{1,0:T(8,128)(2,1)S(1)} %dynamic-slice_bitcast_fusion), channel_id=1, source_target_pairs={{0,1},{1,0},{2,3},{3,2},{4,5},{5,4},{6,7},{7,6},{8,9},{9,8},{10,11... | collective-permute-start | bytes 663560 | tf_op jit(solution)/shard_map/ppermute | solution.py:72
  149.5 16.8 %slice-start = ((s8[5242880]{0:T(1024)(128)(4,1)}), s8[1048576]{0:T(1024)(128)(4,1)S(1)}, s32[]{:S(2)}) async-start(s8[5242880]{0:T(1024)(128)(4,1)} %bitcast.56), calls=%async_computation.6 | async-start | bytes 2097152
  149.5 127.1 %all-to-all-start.1 = ((bf16[16,56,2560]{2,1,0:T(8,128)(2,1)}), bf16[16,56,2560]{2,1,0:T(8,128)(2,1)}, u32[]{:S(2)}, u32[]{:S(2)}) async-start(bf16[16,56,2560]{2,1,0:T(8,128)(2,1)} %bitcast.60), calls=%async_computation.1 | async-start | bytes 9175040 | tf_op jit(solution)/shard_map/all_to_all | solution.py:64
  154.3 98.5 %all-gather.11.cloned.1.call-start = ((), (), s32[]{:S(2)}) async-start(), calls=%async_computation.5 | async-start | bytes 1990656 | tf_op jit(solution)/shard_map/all_gather | solution.py:104
  156.6 9.6 %slice-start.1 = ((s8[5242880]{0:T(1024)(128)(4,1)}), s8[4194304]{0:T(1024)(128)(4,1)S(1)}, s32[]{:S(2)}) async-start(s8[5242880]{0:T(1024)(128)(4,1)} %bitcast.56), calls=%async_computation.7 | async-start | bytes 8388608
  171.1 21.0 %collective-permute-start.3 = (bf16[864,512]{1,0:T(8,128)(2,1)S(1)}, bf16[864,512]{1,0:T(8,128)(2,1)S(1)}, u32[]{:S(2)}, u32[]{:S(2)}) collective-permute-start(bf16[864,512]{1,0:T(8,128)(2,1)S(1)} %constant_dynamic-slice_fusion.1), channel_id=1, source_target_pairs={{0,1},{1,0},{2,3},{3,2},{4,5},{5,4},{6,7},{7,6},{8,9},{9,8},{10,11... | collective-permute-start | bytes 2654216 | tf_op jit(solution)/shard_map/ppermute | solution.py:72
  252.9 9.6 %copy-start.2 = (bf16[1728,512]{1,0:T(8,128)(2,1)S(1)}, bf16[1728,512]{1,0:T(8,128)(2,1)}, u32[]{:S(2)}) copy-start(bf16[1728,512]{1,0:T(8,128)(2,1)} %all-gather.11.cloned.1.call-done) | copy-start | bytes 5308420
  252.9 9.6 %collective-permute-start.4 = (bf16[8,216,512]{2,1,0:T(8,128)(2,1)}, bf16[8,216,512]{2,1,0:T(8,128)(2,1)S(1)}, u32[]{:S(2)}, u32[]{:S(2)}) collective-permute-start(bf16[8,216,512]{2,1,0:T(8,128)(2,1)} %bitcast.64), channel_id=1, source_target_pairs={{0,2},{2,0},{4,6},{6,4},{8,10},{10,8},{12,14},{14,12},{16,18},{18,... | collective-permute-start | bytes 5308424 | tf_op jit(solution)/shard_map/ppermute | solution.py:38
  276.6 111.4 %all-to-all-start.2 = ((bf16[16,56,2560]{2,1,0:T(8,128)(2,1)}), bf16[16,56,2560]{2,1,0:T(8,128)(2,1)}, u32[]{:S(2)}, u32[]{:S(2)}) async-start(bf16[16,56,2560]{2,1,0:T(8,128)(2,1)} %bitcast.61), calls=%async_computation.2 | async-start | bytes 9175040 | tf_op jit(solution)/shard_map/all_to_all | solution.py:64
  298.1 1.2 copy-start.3
  300.3 21.1 %collective-permute-start.5 = (bf16[864,512]{1,0:T(8,128)(2,1)}, bf16[864,512]{1,0:T(8,128)(2,1)}, u32[]{:S(2)}, u32[]{:S(2)}) collective-permute-start(bf16[864,512]{1,0:T(8,128)(2,1)} %constant_dynamic-slice_fusion), channel_id=1, source_target_pairs={{0,1},{1,0},{2,3},{3,2},{4,5},{5,4},{6,7},{7,6},{8,9},{9,8},{10,11... | collective-permute-start | bytes 2654216 | tf_op jit(solution)/shard_map/ppermute | solution.py:72
  301.5 19.9 %copy-start = (f32[864,512]{1,0:T(8,128)S(1)}, f32[864,512]{1,0:T(8,128)}, u32[]{:S(2)}) copy-start(f32[864,512]{1,0:T(8,128)} %convert_add_fusion) | copy-start | bytes 5308420
  302.8 56.5 %collective-permute-start.6 = (bf16[1728,512]{1,0:T(8,128)(2,1)}, bf16[1728,512]{1,0:T(8,128)(2,1)}, u32[]{:S(2)}, u32[]{:S(2)}) collective-permute-start(bf16[1728,512]{1,0:T(8,128)(2,1)} %constant_dynamic-slice_fusion.2), channel_id=1, source_target_pairs={{0,1},{1,0},{2,3},{3,2},{4,5},{5,4},{6,7},{7,6},{8,9},{9,8},{10,11... | collective-permute-start | bytes 5308424 | tf_op jit(solution)/shard_map/ppermute | solution.py:72
  324.4 53.9 %collective-permute-start.7 = (bf16[864,512]{1,0:T(8,128)(2,1)}, bf16[864,512]{1,0:T(8,128)(2,1)}, u32[]{:S(2)}, u32[]{:S(2)}) collective-permute-start(bf16[864,512]{1,0:T(8,128)(2,1)} %multiply_convert_fusion.5), channel_id=1, source_target_pairs={{0,1},{1,0},{2,3},{3,2},{4,5},{5,4},{6,7},{7,6},{8,9},{9,8},{10,11... | collective-permute-start | bytes 2654216 | tf_op jit(solution)/shard_map/ppermute | solution.py:72
Sparse Core Ops, SparseCore 0:
  9.5 32.7 all-gather.6
  43.8 71.3 all-gather.8
  157.9 94.9 all-gather.10
